TPU v7x, 256 devices: a whole 4x4x8 slice. The times are simulated.
256 devices in a mesh: seq: 32 (over z, x_hi, core), dp: 8 (over x_lo, y).
Axes of the slice: x: 4 (x_hi: 2, x_lo: 2; x = x_hi * 2 + x_lo), y: 4, z: 8, core: 2. Of those that a mesh axis runs over, the one named last changes fastest.
Arguments:
- activations: bfloat16 [8, 4096, 768], P('dp', 'seq'), may hold values from -6 to 6
- cotangent: bfloat16 [8, 4096, 768], P('dp', 'seq'), may hold values from -6 to 6
- weights: bfloat16 [3840, 768], P(('seq', 'dp')), may hold values from -0.09375 to 0.09375
- norm_gain: float32 [768], replicated, may hold values from 0.25 to 1.75
- pairing: int32 [768], replicated, may hold values from 0 to 767, as said below
Outputs:
- combined: bfloat16 [8, 4096, 768], P('dp', 'seq')
- grad_input: bfloat16 [8, 4096, 768], P('dp', 'seq')
- grad_kernel: float32 [3840, 768], P(('seq', 'dp'))
- grad_gain: float32 [768], P(('seq', 'dp'))
Inputs may be any that keep to these rules, and one draw needn't show every extreme that they name: pairing is an involution without fixed points: pairing[pairing[c]] = c != pairing[c].
All inputs are finite; a program needn't handle non-finite values.
Results may differ from a plain program's by a relative error of at most 0.0055.
Values may be sent and summed in bfloat16 or wider, within the bound.
A program may use at most 192 MiB of HBM per device.

v0:
```python
import jax
import jax.numpy as jnp
from jax import lax
from jax.sharding import PartitionSpec as P

epsilon = 1e-06


def swapped(block, axis, bit):
    count = lax.axis_size(axis)
    route = []
    for low in range(count):
        high = low | 1 << bit
        if high != low and high < count:
            route += [(low, high), (high, low)]
    return lax.ppermute(block, axis, route)


def padded_2(block, sides, width):
    for axis, dim in sides:
        count = lax.axis_size(axis)
        forward = [(i, i + 1) for i in range(count - 1)]
        backward = [(target, source) for source, target in forward]
        low = lax.ppermute(
            lax.slice_in_dim(block, block.shape[dim] - width, None, axis=dim), axis, forward
        )
        high = lax.ppermute(lax.slice_in_dim(block, 0, width, axis=dim), axis, backward)
        block = jnp.concatenate([low, block, high], axis=dim)
    return block


def reversed_pair(block, pairing):
    return block[:, ::-1][:, :, pairing]


def mirror(stacked, levels):
    mirrored = stacked
    for bit_number in range(levels):
        mirrored = swapped(mirrored, "seq", bit_number)
    return mirrored


def per_device(activations, cotangent, weights, norm_gain, pairing):
    channels = activations.shape[2]
    positions = activations.shape[1]
    gathered = lax.all_gather(weights, ("seq", "dp"), axis=0, tiled=True)
    tap_count = gathered.shape[0] // channels
    kernel_plain = gathered.reshape(tap_count, channels, channels)
    half_cot = 0.5 * cotangent.astype(jnp.float32)
    levels = lax.axis_size("seq").bit_length() - 1
    mirrored = mirror(jnp.stack([activations, cotangent]), levels)
    inputs = [activations, reversed_pair(mirrored[0], pairing)]
    halves = [half_cot, 0.5 * reversed_pair(mirrored[1], pairing).astype(jnp.float32)]
    kernels = [kernel_plain, kernel_plain]
    gain_list = [norm_gain, norm_gain]
    padded = padded_2(jnp.stack(inputs), (("seq", 2),), 2)
    results = []
    windows_list = []
    grad_pres = []
    rms_list = []
    values_list = []
    for strand_index in range(2):
        values_pad = padded[strand_index].astype(jnp.float32)
        inverse_rms = lax.rsqrt(jnp.mean(values_pad * values_pad, -1, keepdims=True) + epsilon)
        normed = (values_pad * inverse_rms * gain_list[strand_index]).astype(jnp.bfloat16)
        windows = jnp.concatenate(
            [normed[:, offset : offset + positions] for offset in range(tap_count)], -1
        )
        flat_kernel = kernels[strand_index].reshape(tap_count * channels, channels)
        preact = jnp.einsum("btk,kd->btd", windows, flat_kernel, preferred_element_type=jnp.float32)
        values = values_pad[:, 2 : 2 + positions]
        results.append(values + jax.nn.gelu(preact))
        _, pullback = jax.vjp(jax.nn.gelu, preact)
        grad_pres.append(pullback(halves[strand_index])[0].astype(jnp.bfloat16))
        windows_list.append(windows)
        rms_list.append(inverse_rms[:, 2 : 2 + positions])
        values_list.append(values)
    grad_padded = padded_2(jnp.stack(grad_pres), (("seq", 2),), 2)
    grad_values = []
    kernel_terms = []
    gain_terms = []
    for strand_index in range(2):
        kernel_terms.append(
            jnp.einsum(
                "btk,btd->kd",
                windows_list[strand_index],
                grad_pres[strand_index],
                preferred_element_type=jnp.float32,
            )
        )
        grad_pad = grad_padded[strand_index]
        back_windows = jnp.concatenate(
            [
                grad_pad[:, tap_count - 1 - offset : tap_count - 1 - offset + positions]
                for offset in range(tap_count)
            ],
            -1,
        )
        kernel_t = kernels[strand_index].transpose(0, 2, 1).reshape(tap_count * channels, channels)
        grad_normed = jnp.einsum(
            "btk,kc->btc", back_windows, kernel_t, preferred_element_type=jnp.float32
        )
        values = values_list[strand_index]
        inverse_rms = rms_list[strand_index]
        gain_terms.append(jnp.sum(grad_normed * values * inverse_rms, (0, 1)))
        scaled = grad_normed * gain_list[strand_index]
        grad_values.append(
            halves[strand_index]
            + inverse_rms * scaled
            - values * inverse_rms**3 * jnp.mean(scaled * values, -1, keepdims=True)
        )
    returned = mirror(
        jnp.stack([results[1].astype(jnp.bfloat16), grad_values[1].astype(jnp.bfloat16)]), levels
    )
    out_round = reversed_pair(returned[0], pairing)
    grad_round = reversed_pair(returned[1], pairing)
    kernel_total = kernel_terms[0] + kernel_terms[1]
    gain_total = gain_terms[0] + gain_terms[1]
    combined = (0.5 * (results[0] + out_round.astype(jnp.float32))).astype(jnp.bfloat16)
    grad_input = (grad_values[0] + grad_round.astype(jnp.float32)).astype(jnp.bfloat16)
    grad_kernel, grad_gain = (
        lax.psum_scatter(kernel_total, ("seq", "dp"), scatter_dimension=0, tiled=True),
        lax.psum_scatter(gain_total, ("seq", "dp"), scatter_dimension=0, tiled=True),
    )
    return (combined, grad_input, grad_kernel, grad_gain)


def solution(mesh):
    placed = (P("dp", "seq", None), P("dp", "seq", None), P(("seq", "dp"), None), P(), P())
    return jax.shard_map(
        per_device,
        mesh=mesh,
        in_specs=placed,
        out_specs=(
            P("dp", "seq", None),
            P("dp", "seq", None),
            P(("seq", "dp"), None),
            P(("seq", "dp")),
        ),
        check_vma=False,
    )
```

profile of v0, /device:TPU:1, one launch (start us, length us, event | category | flops | bytes accessed | tf_op | source)
XLA Modules:
  0.0 1684.6 jit_solution(4556075634723629214)
XLA Ops:
  9.0 3.3 collective-permute-start
  12.3 1.3 collective-permute-done
  14.7 10.8 collective-permute-done.1
  25.4 9.9 collective-permute-done.2
  35.4 1.7 collective-permute-start.3
  37.1 19.3 %collective-permute-done.3 = bf16[2,1,128,768]{3,2,1,0:T(8,128)(2,1)S(1)} collective-permute-done((bf16[2,1,128,768]{3,2,1,0:T(8,128)(2,1)S(1)}, bf16[2,1,128,768]{3,2,1,0:T(8,128)(2,1)S(1)}, u32[]{:S(2)}, u32[]{:S(2)}) %collective-permute-start.3) | collective-permute-done | bytes 393248 | tf_op jit(solution)/shard_map/ppermute | solution.py:16
  56.3 5.1 collective-permute-start.4
  62.1 17.5 %collective-permute-done.4 = bf16[2,1,128,768]{3,2,1,0:T(8,128)(2,1)S(1)} collective-permute-done((bf16[2,1,128,768]{3,2,1,0:T(8,128)(2,1)S(1)}, bf16[2,1,128,768]{3,2,1,0:T(8,128)(2,1)S(1)}, u32[]{:S(2)}, u32[]{:S(2)}) %collective-permute-start.4) | collective-permute-done | bytes 393248 | tf_op jit(solution)/shard_map/ppermute | solution.py:16
  80.0 1.9 gather_fusion
  82.8 3.6 collective-permute-start.5
  86.4 1.9 collective-permute-start.6
  88.7 1.9 gather_fusion.1
  90.8 2.0 collective-permute-done.6
  93.9 647.4 %all-gather.3.cloned.1.call-done = bf16[256,15,768]{2,1,0:T(8,128)(2,1)} async-done(((bf16[1,15,768]{2,1,0:T(8,128)(2,1)}), bf16[256,15,768]{2,1,0:T(8,128)(2,1)}) %all-gather.3.cloned.1.call-update) | async-done | bytes 5898256 | tf_op jit(solution)/shard_map/all_gather | solution.py:46
  741.4 9.6 reshape.400
  750.9 4.8 fusion.19
  755.7 2.0 fusion.26
  757.7 3.5 collective-permute-start.7
  761.2 1.9 collective-permute-start.8
  763.2 9.6 reshape.342
  772.7 9.0 copy.30
  782.4 3.9 fusion.1
  788.2 1.7 collective-permute-done.9
  789.9 5.0 collective-permute-start.10
  794.9 1.7 fusion.8
  796.6 7.6 collective-permute-done.10
  804.2 3.6 collective-permute-start.11
  807.9 6.1 convolution_add_fusion
  814.0 2.3 collective-permute-done.11
  816.2 4.6 collective-permute-start.12
  820.9 683.9 %fusion = f32[16,768]{1,0:T(8,128)S(1)} fusion(f32[3840,768]{1,0:T(8,128)} %convolution_add_fusion), kind=kCustom, calls=%all-reduce-scatter | all-reduce-scatter fusion | flops 3145729 | bytes 11845632
  1504.8 2.1 collective-permute-start.14
  1506.8 1.9 collective-permute-start.15
  1508.8 1.9 collective-permute-start.16
  1513.2 1.9 collective-permute-start.17
  1515.1 23.8 %collective-permute-start.18 = (f32[16,768]{1,0:T(8,128)S(1)}, f32[16,768]{1,0:T(8,128)S(1)}, u32[]{:S(2)}, u32[]{:S(2)}) collective-permute-start(f32[16,768]{1,0:T(8,128)S(1)} %fusion), channel_id=1, source_target_pairs={{0,5},{1,6},{2,7},{3,8},{4,9},{5,10},{6,11},{7,12},{8,13},{9,14},{... | collective-permute-start | bytes 147464
  1538.9 1.9 collective-permute-start.19
  1540.8 1.9 collective-permute-start.20
  1542.8 13.0 collective-permute-start.13
  1555.7 1.9 collective-permute-start.21
  1561.6 2.3 collective-permute-done.21
  1565.2 1.6 collective-permute-start.26
  1566.8 16.1 collective-permute-start.27
  1582.9 12.1 collective-permute-start.28
  1595.1 73.3 %all-reduce.1 = f32[768]{0:T(1024)S(1)} all-reduce(f32[768]{0:T(1024)S(1)} %add.100), channel_id=3, replica_groups=mesh['seq'=32,'dp'=8] {'seq','dp'}, use_global_device_ids=true, to_apply=%region_7.0.clone | all-reduce | flops 768 | bytes 6144
  1668.9 2.1 concatenate.24
  1672.1 1.9 gather_fusion.2
  1674.6 1.9 gather_fusion.3
  (112 shorter events, 20.1 us)
Async XLA Ops:
  7.2 85.6 %copy-start.4 = (bf16[1,128,768]{2,1,0:T(8,128)(2,1)S(1)}, bf16[1,128,768]{2,1,0:T(8,128)(2,1)}, u32[]{:S(2)}) copy-start(bf16[1,128,768]{2,1,0:T(8,128)(2,1)} %param.5) | copy-start | bytes 589828
  7.2 86.0 %copy-start.11 = (f32[768]{0:T(1024)S(1)}, f32[768]{0:T(1024)}, u32[]{:S(2)}) copy-start(f32[768]{0:T(1024)} %param.8) | copy-start | bytes 9220
  7.2 734.2 %all-gather.3.cloned.1.call-start = ((), (), s32[]{:S(2)}) async-start(), calls=%async_computation | async-start | bytes 6316032 | tf_op jit(solution)/shard_map/all_gather | solution.py:46
  9.0 4.6 collective-permute-start
  13.6 11.8 collective-permute-start.1
  25.4 9.9 collective-permute-start.2
  35.4 21.0 %collective-permute-start.3 = (bf16[2,1,128,768]{3,2,1,0:T(8,128)(2,1)S(1)}, bf16[2,1,128,768]{3,2,1,0:T(8,128)(2,1)S(1)}, u32[]{:S(2)}, u32[]{:S(2)}) collective-permute-start(bf16[2,1,128,768]{3,2,1,0:T(8,128)(2,1)S(1)} %collective-permute-done.2), channel_id=1, source_target_pairs={{0,64},{64,0},{8,72},{72,8},{16,80},{80,16},{24,88},{88,24},{32,96... | collective-permute-start | bytes 1179656 | tf_op jit(solution)/shard_map/ppermute | solution.py:16
  56.3 23.2 %collective-permute-start.4 = (bf16[2,1,128,768]{3,2,1,0:T(8,128)(2,1)S(1)}, bf16[2,1,128,768]{3,2,1,0:T(8,128)(2,1)S(1)}, u32[]{:S(2)}, u32[]{:S(2)}) collective-permute-start(bf16[2,1,128,768]{3,2,1,0:T(8,128)(2,1)S(1)} %collective-permute-done.3), channel_id=1, source_target_pairs={{0,128},{128,0},{8,136},{136,8},{16,144},{144,16},{24,152},{152,24... | collective-permute-start | bytes 1179656 | tf_op jit(solution)/shard_map/ppermute | solution.py:16
  82.8 8.0 collective-permute-start.5
  86.4 6.5 collective-permute-start.6
  90.7 664.9 %copy-start.5 = (bf16[768,128]{0,1:T(8,128)(2,1)}, bf16[768,128]{0,1:T(8,128)(2,1)S(1)}, u32[]{:S(2)}) copy-start(bf16[768,128]{0,1:T(8,128)(2,1)S(1)} %copy.29) | copy-start | bytes 589828
  93.9 657.0 %copy-start.7 = (bf16[1,128,768]{2,1,0:T(8,128)(2,1)S(1)}, bf16[1,128,768]{2,1,0:T(8,128)(2,1)}, u32[]{:S(2)}) copy-start(bf16[1,128,768]{2,1,0:T(8,128)(2,1)} %param.6) | copy-start | bytes 589828
  750.9 4.8 copy-start.1
  755.7 26.0 %copy-start.2 = (bf16[1,128,768]{2,1,0:T(8,128)(2,1)}, bf16[1,128,768]{2,1,0:T(8,128)(2,1)S(1)}, u32[]{:S(2)}) copy-start(bf16[1,128,768]{2,1,0:T(8,128)(2,1)S(1)} %get-tuple-element.36) | copy-start | bytes 589828
  757.7 24.1 %collective-permute-start.7 = (bf16[2,1,2,768]{3,2,1,0:T(2,128)(2,1)S(1)}, bf16[2,1,2,768]{3,2,1,0:T(2,128)(2,1)S(1)}, u32[]{:S(2)}, u32[]{:S(2)}) collective-permute-start(bf16[2,1,2,768]{3,2,1,0:T(2,128)(2,1)S(1)} %get-tuple-element.22), channel_id=1, source_target_pairs={{0,8},{8,16},{16,24},{24,32},{32,40},{40,48},{48,56},{56,64},{64,7... | collective-permute-start | bytes 18440 | tf_op jit(solution)/shard_map/ppermute | solution.py:24
  761.2 20.5 %collective-permute-start.8 = (bf16[2,1,2,768]{3,2,1,0:T(2,128)(2,1)S(1)}, bf16[2,1,2,768]{3,2,1,0:T(2,128)(2,1)S(1)}, u32[]{:S(2)}, u32[]{:S(2)}) collective-permute-start(bf16[2,1,2,768]{3,2,1,0:T(2,128)(2,1)S(1)} %get-tuple-element.23), channel_id=1, source_target_pairs={{8,0},{16,8},{24,16},{32,24},{40,32},{48,40},{56,48},{64,56},{72,6... | collective-permute-start | bytes 18440 | tf_op jit(solution)/shard_map/ppermute | solution.py:27
  781.8 4.5 copy-start
  782.4 5.0 copy-start.6
  782.4 5.0 copy-start.9
  786.3 8.6 copy-start.3
  787.9 2.0 collective-permute-start.9
  789.9 14.3 collective-permute-start.10
  804.2 12.0 collective-permute-start.11
  816.2 726.5 %collective-permute-start.12 = (bf16[2,1,128,768]{3,2,1,0:T(8,128)(2,1)}, bf16[2,1,128,768]{3,2,1,0:T(8,128)(2,1)}, u32[]{:S(2)}, u32[]{:S(2)}) collective-permute-start(bf16[2,1,128,768]{3,2,1,0:T(8,128)(2,1)} %collective-permute-done.11), channel_id=1, source_target_pairs={{0,64},{64,0},{8,72},{72,8},{16,80},{80,16},{24,88},{88,24},{32,96... | collective-permute-start | bytes 1179656 | tf_op jit(solution)/shard_map/ppermute | solution.py:16
  1504.8 171.9 %copy-start.8 = (bf16[1,128,768]{2,1,0:T(8,128)(2,1)S(1)}, bf16[1,128,768]{2,1,0:T(8,128)(2,1)}, u32[]{:S(2)}) copy-start(bf16[1,128,768]{2,1,0:T(8,128)(2,1)} %param.6) | copy-start | bytes 589828
  1504.8 171.9 %copy-start.10 = (f32[128,768]{1,0:T(8,128)S(1)}, f32[128,768]{1,0:T(8,128)}, u32[]{:S(2)}) copy-start(f32[128,768]{1,0:T(8,128)} %get-tuple-element.37) | copy-start | bytes 1179652
  1504.8 10.3 collective-permute-start.14
  1506.8 32.1 %collective-permute-start.15 = (f32[16,768]{1,0:T(8,128)S(1)}, f32[16,768]{1,0:T(8,128)S(1)}, u32[]{:S(2)}, u32[]{:S(2)}) collective-permute-start(f32[16,768]{1,0:T(8,128)S(1)} %fusion), channel_id=1, source_target_pairs={{0,2},{1,3},{2,4},{3,5},{4,6},{5,7},{6,8},{7,9},{8,10},{9,11},{10,... | collective-permute-start | bytes 147464
  1508.8 32.1 %collective-permute-start.16 = (f32[16,768]{1,0:T(8,128)S(1)}, f32[16,768]{1,0:T(8,128)S(1)}, u32[]{:S(2)}, u32[]{:S(2)}) collective-permute-start(f32[16,768]{1,0:T(8,128)S(1)} %fusion), channel_id=1, source_target_pairs={{0,3},{1,4},{2,5},{3,6},{4,7},{5,8},{6,9},{7,10},{8,11},{9,12},{10... | collective-permute-start | bytes 147464
  1510.7 2.5 collective-permute-start.29
  1513.2 42.6 %collective-permute-start.17 = (f32[16,768]{1,0:T(8,128)S(1)}, f32[16,768]{1,0:T(8,128)S(1)}, u32[]{:S(2)}, u32[]{:S(2)}) collective-permute-start(f32[16,768]{1,0:T(8,128)S(1)} %fusion), channel_id=1, source_target_pairs={{0,4},{1,5},{2,6},{3,7},{4,8},{5,9},{6,10},{7,11},{8,12},{9,13},{1... | collective-permute-start | bytes 147464
  1515.1 42.6 %collective-permute-start.18 = (f32[16,768]{1,0:T(8,128)S(1)}, f32[16,768]{1,0:T(8,128)S(1)}, u32[]{:S(2)}, u32[]{:S(2)}) collective-permute-start(f32[16,768]{1,0:T(8,128)S(1)} %fusion), channel_id=1, source_target_pairs={{0,5},{1,6},{2,7},{3,8},{4,9},{5,10},{6,11},{7,12},{8,13},{9,14},{... | collective-permute-start | bytes 147464
  1538.9 20.1 %collective-permute-start.19 = (f32[16,768]{1,0:T(8,128)S(1)}, f32[16,768]{1,0:T(8,128)S(1)}, u32[]{:S(2)}, u32[]{:S(2)}) collective-permute-start(f32[16,768]{1,0:T(8,128)S(1)} %fusion), channel_id=1, source_target_pairs={{0,6},{1,7},{2,8},{3,9},{4,10},{5,11},{6,12},{7,13},{8,14},{9,15},... | collective-permute-start | bytes 147464
  1540.8 19.4 %collective-permute-start.20 = (f32[16,768]{1,0:T(8,128)S(1)}, f32[16,768]{1,0:T(8,128)S(1)}, u32[]{:S(2)}, u32[]{:S(2)}) collective-permute-start(f32[16,768]{1,0:T(8,128)S(1)} %fusion), channel_id=1, source_target_pairs={{0,7},{1,8},{2,9},{3,10},{4,11},{5,12},{6,13},{7,14},{8,15},{9,16}... | collective-permute-start | bytes 147464
  1542.8 128.9 %collective-permute-start.13 = (bf16[2,1,128,768]{3,2,1,0:T(8,128)(2,1)}, bf16[2,1,128,768]{3,2,1,0:T(8,128)(2,1)S(1)}, u32[]{:S(2)}, u32[]{:S(2)}) collective-permute-start(bf16[2,1,128,768]{3,2,1,0:T(8,128)(2,1)} %collective-permute-done.12), channel_id=1, source_target_pairs={{0,128},{128,0},{8,136},{136,8},{16,144},{144,16},{24,152},{152,24... | collective-permute-start | bytes 1179656 | tf_op jit(solution)/shard_map/ppermute | solution.py:16
  1555.7 8.2 collective-permute-start.21
  1557.7 7.6 collective-permute-start.22
  1559.0 7.9 collective-permute-start.23
  1560.3 22.6 %collective-permute-start.24 = (f32[16,768]{1,0:T(8,128)S(1)}, f32[16,768]{1,0:T(8,128)S(1)}, u32[]{:S(2)}, u32[]{:S(2)}) collective-permute-start(f32[16,768]{1,0:T(8,128)S(1)} %fusion), channel_id=1, source_target_pairs={{0,11},{1,12},{2,13},{3,14},{4,15},{5,16},{6,17},{7,18},{8,19},{9,... | collective-permute-start | bytes 147464
  1563.9 105.0 %collective-permute-start.25 = (f32[16,768]{1,0:T(8,128)S(1)}, f32[16,768]{1,0:T(8,128)S(1)}, u32[]{:S(2)}, u32[]{:S(2)}) collective-permute-start(f32[16,768]{1,0:T(8,128)S(1)} %fusion), channel_id=1, source_target_pairs={{0,12},{1,13},{2,14},{3,15},{4,16},{5,17},{6,18},{7,19},{8,20},{9,... | collective-permute-start | bytes 147464
  1565.2 103.7 %collective-permute-start.26 = (f32[16,768]{1,0:T(8,128)S(1)}, f32[16,768]{1,0:T(8,128)S(1)}, u32[]{:S(2)}, u32[]{:S(2)}) collective-permute-start(f32[16,768]{1,0:T(8,128)S(1)} %fusion), channel_id=1, source_target_pairs={{0,13},{1,14},{2,15},{3,16},{4,17},{5,18},{6,19},{7,20},{8,21},{9,... | collective-permute-start | bytes 147464
  1566.8 102.1 %collective-permute-start.27 = (f32[16,768]{1,0:T(8,128)S(1)}, f32[16,768]{1,0:T(8,128)S(1)}, u32[]{:S(2)}, u32[]{:S(2)}) collective-permute-start(f32[16,768]{1,0:T(8,128)S(1)} %fusion), channel_id=1, source_target_pairs={{0,14},{1,15},{2,16},{3,17},{4,18},{5,19},{6,20},{7,21},{8,22},{9,... | collective-permute-start | bytes 147464
  1582.9 86.0 %collective-permute-start.28 = (f32[16,768]{1,0:T(8,128)S(1)}, f32[16,768]{1,0:T(8,128)S(1)}, u32[]{:S(2)}, u32[]{:S(2)}) collective-permute-start(f32[16,768]{1,0:T(8,128)S(1)} %fusion), channel_id=1, source_target_pairs={{0,15},{1,16},{2,17},{3,18},{4,19},{5,20},{6,21},{7,22},{8,23},{9,... | collective-permute-start | bytes 147464
Sparse Core Ops, SparseCore 0:
  9.9 731.4 all-gather.2
where the time goes:
time: 1690 us; the launch traced here: 1680 us
  blocking collectives  757 us (45%)
  waiting for transfers between devices  724 us (43%)
  starting transfers between devices  122 us (7%)
  local copies, waits for them, and re-layouts  42.1 us (2%)
  matrix products  19.5 us (1%)
    unnamed x2, blocking collectives  757 us
    all_gather x1, waiting for transfers between devices, per_device(): gathered = lax.all_gather(weights, ('seq', 'dp'), axis=0, tiled=True)  647 us
    unnamed x16, starting transfers between devices  73.6 us
    ppermute x10, waiting for transfers between devices, swapped(): return lax.ppermute(block, axis, route)  70.4 us
    ppermute x10, starting transfers between devices, swapped(): return lax.ppermute(block, axis, route)  37.6 us
  transfers between devices with their start and end apart: 31, of which 12 were waited for; matrix products, arithmetic and copies ran while one was open for 43% of the time, Pallas kernels for 0%

commit v1 on v0

v1 whole, which is shorter than its diff:
```python
import functools

import jax
import jax.numpy as jnp
from jax import lax
from jax.experimental import pallas as pl
from jax.experimental.pallas import tpu as pltpu
from jax.sharding import PartitionSpec as P

EPS = 1e-06
MESH = pl.DeviceIdType.MESH
BF = jnp.bfloat16
F32 = jnp.float32

C = 768
HALF = 384
OWN = 128
TAPS = 5
ROWS = 288
CHIP0 = 16
NZ, NX, NY = 8, 4, 4
MSGS = 128


def rem(a, n):
    return lax.rem(a, jnp.int32(n))


def div(a, n):
    return lax.div(a, jnp.int32(n))


def place(z, x, y, c):
    return (z * 4 + div(x, 2) * 2 + c, rem(x, 2) * 4 + y)


def loop(count, body):
    def step(i, carry):
        body(i)
        return carry

    lax.fori_loop(0, count, step, 0)


def dot(a, b):
    return jnp.dot(a, b, preferred_element_type=F32)


def dot_nt(a, b):
    return lax.dot_general(a, b, (((1,), (1,)), ((), ())), preferred_element_type=F32)


def gelu_parts(x):
    k = 0.7978845608028654
    x2 = x * x
    t = jnp.tanh(k * (x + 0.044715 * x2 * x))
    cdf = 0.5 * (1.0 + t)
    slope = cdf + x * (0.5 * (1.0 - t * t)) * (k * (1.0 + 3 * 0.044715 * x2))
    return x * cdf, slope


def kernel(
    act, cot, wsh, gain, pairing,
    out_ref, grad_ref, gk_ref, gg_ref,
    xe, ce, xp, cp, perm, perm_half, inv_ref, nf, wnd, wp, wpt, wb, dwb, acc,
    resf, resr, gpf, gpb, wun, gnb, gnx, rfx, rrx,
    slot4, slot8, red4, red8, slot_y, slot_x, slot_2x, one01, one2, slot_z, slot_2y,
    gsum, gz, gx, gy, gp_, fin, finx,
    send, recv, local, halo,
):
    s = lax.axis_index("seq")
    d = lax.axis_index("dp")
    z, xh, core = div(s, 4), rem(div(s, 2), 2), rem(s, 2)
    xl, y = div(d, 4), rem(d, 4)
    x = xh * 2 + xl
    m = z * 2 + xh
    other = 1 - core

    def in_x(o):
        return place(z, rem(x + o, NX), y, core)

    def in_y(o):
        return place(z, x, rem(y + o, NY), core)

    def in_z(o):
        return place(rem(z + o, NZ), x, y, core)

    partner = place(z, x, y, other)

    def chip_m(mm, c):
        return place(div(mm, 2), rem(mm, 2) * 2 + xl, y, c)

    barrier = pltpu.get_barrier_semaphore()
    met = [partner]
    met += [in_x(o) for o in range(1, NX)] + [in_y(o) for o in range(1, NY)]
    met += [in_z(o) for o in range(1, NZ)]
    met += [chip_m(rem(m + o, 16), c) for o in (1, 15) for c in (0, 1)]
    for who in met:
        pl.semaphore_signal(barrier, inc=1, device_id=who, device_id_type=MESH)
    pl.semaphore_wait(barrier, len(met))

    started = []

    def put(src, dst, who):
        i = len(started)
        copy = pltpu.make_async_remote_copy(
            src_ref=src, dst_ref=dst, send_sem=send.at[i], recv_sem=recv.at[i],
            device_id=who, device_id_type=MESH,
        )
        copy.start()
        started.append(copy)
        return copy

    def keep(src, dst, i):
        copy = pltpu.make_async_copy(src, dst, local.at[i])
        copy.start()
        return copy

    mine16 = pl.ds(pl.multiple_of(core * 16, 16), 16)
    mine = pl.ds(pl.multiple_of(CHIP0 + core * OWN, 16), OWN)
    theirs = pl.ds(pl.multiple_of(CHIP0 + other * OWN, 16), OWN)
    w_there = put(wsh.at[other], wb.at[:, z, x, y, mine16, :], partner)
    w_here = keep(wsh.at[core], wb.at[:, z, x, y, mine16, :], 0)
    x_here = keep(act.at[0], xe.at[mine], 1)
    c_here = keep(cot.at[0], ce.at[mine], 2)
    x_there = put(act.at[0], xe.at[mine], partner)
    edge_src = pl.ds(pl.multiple_of(core * 112, 16), 16)
    edge_dst = pl.ds(pl.multiple_of(other * 272, 16), 16)
    toward = rem(m + core * 2 + 15, 16)
    edges = []
    for c in (0, 1):
        for k, (src, dst) in enumerate(((act, xe), (cot, ce))):
            i = len(edges)
            copy = pltpu.make_async_remote_copy(
                src_ref=src.at[0, edge_src], dst_ref=dst.at[edge_dst],
                send_sem=halo.at[2 + i, 0], recv_sem=halo.at[k, core],
                device_id=chip_m(toward, c), device_id_type=MESH,
            )
            copy.start()
            edges.append(copy)
    c_there = put(cot.at[0], ce.at[mine], partner)

    w_here.wait()
    w_there.wait_recv()
    first01 = [
        put(wb.at[pl.ds(0, 2), z, x, y], wb.at[pl.ds(0, 2), z, x, y], in_z(o)) for o in range(1, NZ)
    ]
    first2 = [put(wb.at[2, z, x, y], wb.at[2, z, x, y], in_y(o)) for o in range(1, NY)]

    perm[...] = (lax.broadcasted_iota(jnp.int32, (C, C), 0) == pairing[...]).astype(F32).astype(BF)
    half_cols = pl.ds(pl.multiple_of(core * HALF, 128), HALF)
    other_cols = pl.ds(pl.multiple_of(other * HALF, 128), HALF)
    perm_half[...] = (
        (lax.broadcasted_iota(jnp.int32, (C, HALF), 0) == pairing[:, half_cols])
        .astype(F32).astype(BF)
    )

    x_here.wait()
    c_here.wait()
    x_there.wait_recv()
    c_there.wait_recv()
    for k, dst in enumerate((xe, ce)):
        for side in (0, 1):
            into = dst.at[pl.ds(272 * (1 - side), 16)]
            pltpu.make_async_remote_copy(
                src_ref=into, dst_ref=into, send_sem=halo.at[2, 0], recv_sem=halo.at[k, side],
                device_id=partner, device_id_type=MESH,
            ).wait_recv()

    def inside(first, count, width):
        row = lax.broadcasted_iota(jnp.int32, (count, width), 0) + first
        low = jnp.where(m > 0, 0, CHIP0)
        high = jnp.where(m < 15, ROWS, ROWS - 16)
        return (row >= low) & (row < high)

    def norm_rows(i):
        at = pl.ds(pl.multiple_of(i * 32, 32), 32)
        raw = xe[at, :]
        values = jnp.where(inside(i * 32, 32, C), raw.astype(F32), 0.0)
        inverse = lax.rsqrt(jnp.mean(values * values, -1, keepdims=True) + EPS)
        inv_ref[at, :] = inverse
        swapped = dot(values.astype(BF), perm[...])
        xp[at, :] = swapped.astype(BF)
        into = pl.ds(pl.multiple_of(8 + i * 32, 8), 32)
        nf[0, into, :] = (values * inverse * gain[...]).astype(BF).astype(F32)
        nf[1, into, :] = (swapped * inverse * gain[...]).astype(BF).astype(F32)
        cp[at, :] = dot(ce[at, :], perm[...]).astype(BF)

    nf[:, 0:8, :] = jnp.zeros((2, 8, C), F32)
    nf[:, 8 + ROWS :, :] = jnp.zeros((2, 8, C), F32)
    wnd[:, TAPS * C :] = jnp.zeros((2 * ROWS, 128), BF)
    loop(ROWS // 32, norm_rows)

    for copy in first2:
        copy.wait_recv()
    second2 = [put(wb.at[2, z, x], wb.at[2, z, x], in_x(o)) for o in range(1, NX)]

    def window_cols(i):
        cols = pl.ds(pl.multiple_of(i * 128, 128), 128)
        for strand in (0, 1):
            for k in range(TAPS):
                shift = (k - 2) if strand == 0 else (2 - k)
                wnd[strand * ROWS : (strand + 1) * ROWS, pl.ds(pl.multiple_of(k * C + i * 128, 128), 128)] = nf[
                    strand, 8 + shift : 8 + shift + ROWS, cols
                ].astype(BF)

    loop(C // 128, window_cols)

    for copy in first01:
        copy.wait_recv()
    second0 = [put(wb.at[0, :, x, y], wb.at[0, :, x, y], in_y(o)) for o in range(1, NY)]
    second1 = [put(wb.at[1, :, x, y], wb.at[1, :, x, y], in_x(o)) for o in range(1, NX)]

    def source_of(slot, g):
        r = slot & 15
        c, yy, xx = (slot >> 4) & 1, (slot >> 5) & 3, slot >> 7
        src = ((c * 2 + xx) * 4 + yy) * 15 + r + 16 * rem(15 * g, 8)
        return jnp.where(r < 15, src, -1)

    def iota(shape, axis):
        return lax.broadcasted_iota(jnp.int32, shape, axis)

    def onehot(flag):
        return flag.astype(F32).astype(BF)

    def pad_group(g):
        cols = pl.ds(pl.multiple_of(div(15 * g, 8) * 128, 128), 384)
        spread = onehot(iota((384, 256), 0) == source_of(iota((384, 256), 1), g))
        into = pl.ds(pl.multiple_of(g * 256, 256), 256)
        wp[:, into] = dot(wnd[:, cols], spread).astype(BF)

    def pad_group_t(g):
        cols = pl.ds(pl.multiple_of(div(15 * g, 8) * 128, 128), 384)
        spread = onehot(iota((256, 384), 1) == source_of(iota((256, 384), 0), g))
        into = pl.ds(pl.multiple_of(g * 256, 256), 256)
        for strand in (0, 1):
            rows = slice(strand * ROWS + CHIP0, strand * ROWS + CHIP0 + 256)
            wpt[into, strand * 256 : (strand + 1) * 256] = dot_nt(spread, wnd[rows, cols]).astype(BF)

    loop(16, pad_group)

    def part(ref, colour, coord, half):
        if colour == 0:
            return ref.at[0, pl.ds(half * 4, 4), coord]
        if colour == 1:
            return ref.at[1, pl.ds(half * 4, 4), :, coord]
        return ref.at[2, coord, pl.ds(half * 2, 2)]

    rings = ((x, NX, in_x), (y, NY, in_y), (z, NZ, in_z))

    def limit(n, sign, half):
        return n // 2 if (half == 0) == (sign == 1) else n // 2 - 1

    def ring_send(colour, sign, half, hop):
        q, n, who = rings[colour]
        held = part(wb, colour, rem(q - sign * (hop - 1) + n, n), half)
        return put(held, held, who(1 if sign == 1 else n - 1))

    ways = ((1, 0), (-1, 1), (1, 1), (-1, 0))

    for copy in second2:
        copy.wait_recv()
    live = {}
    for sign, half in ways:
        live[2, sign, half] = ring_send(2, sign, half, 1)
    for copy in second0:
        copy.wait_recv()
    for sign, half in ways:
        live[0, sign, half] = ring_send(0, sign, half, 1)
    for copy in second1:
        copy.wait_recv()
    for sign, half in ways:
        live[1, sign, half] = ring_send(1, sign, half, 1)

    loop(16, pad_group_t)

    for hop in range(1, NZ // 2 + 1):
        for colour in (2, 0, 1):
            n = rings[colour][1]
            for sign, half in ways:
                if hop > limit(n, sign, half):
                    continue
                live[colour, sign, half].wait_recv()
                if hop < limit(n, sign, half):
                    live[colour, sign, half] = ring_send(colour, sign, half, hop + 1)

    def weights(i, groups):
        pieces = []
        for colour in range(3):
            got = wb[colour].reshape(16, 2 * NY * 64, 128) if groups is None else None
            pieces.append(got)
        return pieces

    def group_of(ref, zz, first):
        return jnp.concatenate(
            [ref[j, zz, pl.ds(first, 2)].reshape(256, 128) for j in range(3)], axis=1
        )

    def forward_rows(zz):
        right = jnp.concatenate(
            [wb[j, zz].reshape(512, 128) for j in range(3)], axis=1
        )
        return dot(wp[:, pl.ds(pl.multiple_of(zz * 512, 512), 512)], right)

    acc[...] = jnp.zeros((2 * ROWS, HALF), F32)

    def forward_step(zz):
        acc[...] += forward_rows(zz)

    loop(NZ, forward_step)

    def gelu_rows(strand):
        def body(i):
            at = pl.ds(pl.multiple_of(i * 32, 32), 32)
            pre = acc[pl.ds(pl.multiple_of(strand * ROWS + i * 32, 32), 32), :]
            value, slope = gelu_parts(pre)
            if strand == 0:
                resf[at, :] = xe[at, half_cols].astype(F32) + value
                g = ce[at, half_cols].astype(F32)
            else:
                resr[at, :] = (xp[at, half_cols].astype(F32) + value).astype(BF)
                g = cp[at, half_cols].astype(F32)
            gp = jnp.where(inside(i * 32, 32, HALF), 0.5 * g * slope, 0.0).astype(BF)
            gpb[strand, at, :] = gp
            gpf[strand, pl.ds(pl.multiple_of(8 + i * 32, 8), 32), :] = gp.astype(F32)

        return body

    loop(ROWS // 32, gelu_rows(0))
    loop(ROWS // 32, gelu_rows(1))

    def dw_group(g):
        zz, hh = div(g, 2), rem(g, 2) * 2
        right = jnp.concatenate(
            [gpb[0, CHIP0 : CHIP0 + 256, :], gpb[1, CHIP0 : CHIP0 + 256, :]], axis=0
        )
        got = dot(wpt[pl.ds(pl.multiple_of(g * 256, 256), 256), :], right).astype(BF)
        for j in range(3):
            dwb[j, zz, pl.ds(hh, 2)] = got[:, j * 128 : (j + 1) * 128].reshape(2, NY, 32, 128)

    loop(16, dw_group)

    def ring_slot(colour, sign, half, dist):
        way = ways.index((sign, half))
        if colour == 2:
            return slot8.at[way, dist - 1]
        return slot4.at[colour, way, dist - 1]

    def ring_give(colour, sign, half, dist, src):
        q, n, who = rings[colour]
        return put(src, ring_slot(colour, sign, half, dist), who(1 if sign == 1 else n - 1))

    for colour in (2, 0, 1):
        q, n, who = rings[colour]
        for sign, half in ways:
            dist = limit(n, sign, half)
            src = part(dwb, colour, rem(q + sign * dist + n, n), half)
            live[colour, sign, half] = ring_give(colour, sign, half, dist, src)

    there = pl.ds(pl.multiple_of(CHIP0 + other * OWN, 16), OWN)
    f_there = put(resf.at[there], rfx, partner)
    r_there = put(resr.at[there], rrx, partner)

    def pack_group(g):
        zz, hh = div(g, 2), rem(g, 2) * 2
        gather = onehot(iota((240, 256), 0) == source_of(iota((240, 256), 1), 0))
        right = group_of(wb, zz, hh)
        wun[pl.ds(pl.multiple_of(g * 240, 16), 240), :] = dot(gather, right).astype(BF)

    def ring_step(colour, hop):
        q, n, who = rings[colour]
        for sign, half in ways:
            dist = limit(n, sign, half) - (hop - 1)
            if dist < 1:
                continue
            live[colour, sign, half].wait_recv()
            if dist > 1:
                got = ring_slot(colour, sign, half, dist)
                add = part(dwb, colour, rem(q + sign * (dist - 1) + n, n), half)
                got[...] = (got[...].astype(F32) + add[...].astype(F32)).astype(BF)
                live[colour, sign, half] = ring_give(colour, sign, half, dist - 1, got)

    def ring_total(colour, half):
        q = rings[colour][0]
        total = part(dwb, colour, q, half)[...].astype(F32)
        for sign in (1, -1):
            total = total + ring_slot(colour, sign, half, 1)[...].astype(F32)
        return total.astype(BF)

    loop(16, pack_group)

    ring_step(2, 1)
    ring_step(0, 1)
    ring_step(1, 1)

    gpf[:, 0:8, :] = jnp.zeros((2, 8, HALF), F32)
    gpf[:, 8 + ROWS :, :] = jnp.zeros((2, 8, HALF), F32)

    def normed_grad(block):
        first = 8 + CHIP0 + block * OWN
        for strand in (0, 1):
            total = None
            for k in range(TAPS):
                shift = (2 - k) if strand == 0 else (k - 2)
                left = gpf[strand, first + shift : first + shift + OWN, :].astype(BF)
                term = dot_nt(left, wun[k * C : (k + 1) * C, :])
                total = term if total is None else total + term
            gnb[block, strand] = total

    normed_grad(0)
    ring_step(2, 2)
    ring_step(0, 2)
    ring_step(1, 2)
    red4[0, 0:4] = ring_total(0, 0)
    red4[0, 4:8] = ring_total(0, 1)
    red4[1, 0:4] = ring_total(1, 0)
    red4[1, 4:8] = ring_total(1, 1)
    part0 = [put(red4.at[0, :, rem(y + o, NY)], slot_y.at[o - 1], in_y(o)) for o in range(1, NY)]
    part1 = [put(red4.at[1, :, rem(x + o, NX)], slot_x.at[o - 1], in_x(o)) for o in range(1, NX)]
    normed_grad(1)
    ring_step(2, 3)
    n_there = put(gnb.at[other], gnx, partner)

    ring_step(2, 4)
    red8[0:2] = ring_total(2, 0)
    red8[2:4] = ring_total(2, 1)
    part2 = [put(red8.at[rem(x + o, NX)], slot_2x.at[o - 1], in_x(o)) for o in range(1, NX)]

    n_there.wait_recv()
    f_there.wait_recv()
    r_there.wait_recv()
    gsum[...] = jnp.zeros((8, 128), F32)

    def finish_rows(i, carry):
        own = pl.ds(pl.multiple_of(i * 32, 32), 32)
        at = pl.ds(pl.multiple_of(CHIP0 + core * OWN + i * 32, 16), 32)
        inverse = inv_ref[at, :]
        v, vp = xe[at, :].astype(F32), xp[at, :].astype(F32)
        gn = gnb[core, 0, own, :] + gnx[0, own, :]
        gr = gnb[core, 1, own, :] + gnx[1, own, :]
        term = gn * v * inverse + gr * vp * inverse
        cube = inverse * inverse * inverse
        sf, sr = gn * gain[...], gr * gain[...]
        grad_f = 0.5 * ce[at, :].astype(F32) + inverse * sf - v * (cube * jnp.mean(sf * v, -1, keepdims=True))
        grad_r = 0.5 * cp[at, :].astype(F32) + inverse * sr - vp * (cube * jnp.mean(sr * vp, -1, keepdims=True))
        back = dot(grad_r.astype(BF), perm[...])
        grad_ref[own, :] = (grad_f + back).astype(BF)
        mine_f, mine_r = resf[at, :], resr[at, :]
        their_f, their_r = rfx[own, :], rrx[own, :]
        low = core == 0
        full_f = jnp.concatenate(
            [jnp.where(low, mine_f, their_f), jnp.where(low, their_f, mine_f)], axis=1
        )
        mr, tr = mine_r.astype(F32), their_r.astype(F32)
        full_r = jnp.concatenate([jnp.where(low, mr, tr), jnp.where(low, tr, mr)], axis=1)
        back_r = dot(full_r.astype(BF), perm[...])
        out_ref[own, :] = (0.5 * (full_f + back_r)).astype(BF)
        return carry + jnp.sum(term, 0, keepdims=True)

    gain_part = lax.fori_loop(0, OWN // 32, finish_rows, jnp.zeros((1, C), F32))
    for j in range(C // 128):
        gsum[j : j + 1, :] = gain_part[:, j * 128 : (j + 1) * 128]
    to_z = [put(gsum, gz.at[o - 1], in_z(o)) for o in range(1, NZ)]

    def gathered(own, slots):
        total = own
        for o in range(len(slots)):
            total = total + slots[o]
        return total

    for copy in part0 + part1:
        copy.wait_recv()
    one01[:, 0] = gathered(
        red4[0, :, y].astype(F32), [slot_y[o].astype(F32) for o in range(NY - 1)]
    ).astype(BF)
    one01[:, 1] = gathered(
        red4[1, :, x].astype(F32), [slot_x[o].astype(F32) for o in range(NX - 1)]
    ).astype(BF)
    last01 = [put(one01.at[rem(z + o, NZ)], slot_z.at[o - 1], in_z(o)) for o in range(1, NZ)]

    for copy in part2:
        copy.wait_recv()
    one2[...] = gathered(
        red8[x].astype(F32), [slot_2x[o].astype(F32) for o in range(NX - 1)]
    ).astype(BF)
    last2 = [put(one2.at[rem(y + o, NY)], slot_2y.at[o - 1], in_y(o)) for o in range(1, NY)]

    for copy in to_z:
        copy.wait_recv()
    gp_[0] = gathered(gsum[...], [gz[o] for o in range(NZ - 1)])
    to_x = [put(gp_.at[0], gx.at[o - 1], in_x(o)) for o in range(1, NX)]

    for copy in last2:
        copy.wait_recv()
    fin[:, 256:384] = gathered(
        one2[y].astype(F32), [slot_2y[o].astype(F32) for o in range(NY - 1)]
    )
    for copy in to_x:
        copy.wait_recv()
    gp_[1] = gathered(gp_[0], [gx[o] for o in range(NX - 1)])
    to_y = [put(gp_.at[1], gy.at[o - 1], in_y(o)) for o in range(1, NY)]
    for copy in last01:
        copy.wait_recv()
    for j in (0, 1):
        fin[:, j * 128 : (j + 1) * 128] = gathered(
            one01[z, j].astype(F32), [slot_z[o, j].astype(F32) for o in range(NZ - 1)]
        )
    theirs16 = pl.ds(pl.multiple_of(other * 16, 16), 16)
    fin_there = put(fin.at[theirs16], finx, partner)
    for copy in to_y:
        copy.wait_recv()
    gp_[2] = gathered(gp_[1], [gy[o] for o in range(NY - 1)])
    gain_there = put(gp_.at[2], gp_.at[3], partner)
    gk_ref[:, half_cols] = fin[mine16, :]
    fin_there.wait_recv()
    gk_ref[:, other_cols] = finx[...]
    gain_there.wait_recv()
    total = gp_[2] + gp_[3]
    flat = iota((8, 128), 0) * 128 + iota((8, 128), 1)
    picked = jnp.zeros((8, 128), F32)
    for j in range(3):
        chosen = jnp.where(flat == (s * 8 + d) * 3 + j, total, 0.0)
        value = jnp.sum(jnp.sum(chosen, 1, keepdims=True), 0, keepdims=True)
        picked = jnp.where(iota((8, 128), 1) == j, value, picked)
    gg_ref[...] = picked

    for copy in started:
        copy.wait_send()
    for copy in edges:
        copy.wait_send()


def scratch():
    v = pltpu.VMEM
    dma = pltpu.SemaphoreType.DMA
    return [
        v((ROWS, C), BF), v((ROWS, C), BF), v((ROWS, C), BF), v((ROWS, C), BF),
        v((C, C), BF), v((C, HALF), BF), v((ROWS, 1), F32),
        v((2, ROWS + 16, C), F32), v((2 * ROWS, TAPS * C + 128), BF),
        v((2 * ROWS, 4096), BF), v((4096, 512), BF),
        v((3, NZ, NX, NY, 32, 128), BF), v((3, NZ, NX, NY, 32, 128), BF),
        v((2 * ROWS, HALF), F32), v((ROWS, HALF), F32), v((ROWS, HALF), BF),
        v((2, ROWS + 16, HALF), F32), v((2, ROWS, HALF), BF),
        v((TAPS * C, HALF), BF),
        v((2, 2, OWN, C), F32), v((2, OWN, C), F32),
        v((OWN, HALF), F32), v((OWN, HALF), BF),
        v((2, 4, 2, 4, 4, 32, 128), BF), v((4, 4, 2, NY, 32, 128), BF),
        v((2, NZ, 4, 32, 128), BF), v((NX, NY, 32, 128), BF),
        v((3, NZ, 32, 128), BF), v((3, NZ, 32, 128), BF),
        v((3, NY, 32, 128), BF),
        v((NZ, 2, 32, 128), BF), v((NY, 32, 128), BF),
        v((7, 2, 32, 128), BF), v((3, 32, 128), BF),
        v((8, 128), F32), v((7, 8, 128), F32), v((3, 8, 128), F32), v((3, 8, 128), F32),
        v((4, 8, 128), F32),
        v((32, HALF), F32), v((16, HALF), F32),
        dma((MSGS,)), dma((MSGS,)), dma((3,)), dma((6, 2)),
    ]


def per_device(activations, cotangent, weights, norm_gain, pairing):
    padded = jnp.pad(weights, ((0, 1), (0, 0))).reshape(16, 2, 3, 128).transpose(1, 2, 0, 3)
    vmem = pl.BlockSpec(memory_space=pltpu.VMEM)
    anywhere = pl.BlockSpec(memory_space=pl.ANY)
    combined, grad_input, grad_kernel, grad_gain = pl.pallas_call(
        kernel,
        out_shape=(
            jax.ShapeDtypeStruct((OWN, C), BF),
            jax.ShapeDtypeStruct((OWN, C), BF),
            jax.ShapeDtypeStruct((16, C), F32),
            jax.ShapeDtypeStruct((8, 128), F32),
        ),
        in_specs=[anywhere, anywhere, vmem, vmem, vmem],
        out_specs=(vmem, vmem, vmem, vmem),
        scratch_shapes=scratch(),
        compiler_params=pltpu.CompilerParams(
            collective_id=0, has_side_effects=True, vmem_limit_bytes=60 * 2**20
        ),
        name="strands",
    )(activations, cotangent, padded, norm_gain.reshape(1, C), pairing.reshape(1, C))
    return combined[None], grad_input[None], grad_kernel[:15], grad_gain[0, :3]


def solution(mesh):
    placed = (P("dp", "seq", None), P("dp", "seq", None), P(("seq", "dp"), None), P(), P())
    return jax.shard_map(
        per_device,
        mesh=mesh,
        in_specs=placed,
        out_specs=(
            P("dp", "seq", None),
            P("dp", "seq", None),
            P(("seq", "dp"), None),
            P(("seq", "dp")),
        ),
        check_vma=False,
    )
```

time: 1690 us -> 103 us (0.06)
  blocking collectives: 757 us -> 0 us
  waiting for transfers between devices: 724 us -> 0 us
  starting transfers between devices: 122 us -> 0 us
  Pallas kernels: 0 us -> 94.2 us
  local copies, waits for them, and re-layouts: 42.1 us -> 7.5 us
  matrix products: 19.5 us -> 0 us
    unnamed x2 -> x0, blocking collectives: 757 us -> none
    all_gather x1 -> x0, waiting for transfers between devices: 647 us -> none  [per_device(): gathered = lax.all_gather(weights, ('seq', 'dp'), axis=0, tiled=True)]
    pallas_call x0 -> x1, Pallas kernels: none -> 94.2 us  [per_device(): pl.pallas_call(kernel, out_shape=(jax.ShapeDtypeStruct((OWN, C), BF), jax...]
    unnamed x16 -> x0, starting transfers between devices: 73.6 us -> none
    ppermute x14 -> x0, waiting for transfers between devices: 72.5 us -> none  [the longest x10 70.4 us: swapped(): return lax.ppermute(block, axis, route)]
    ppermute x14 -> x0, starting transfers between devices: 48.5 us -> none  [the longest x10 37.6 us: swapped(): return lax.ppermute(block, axis, route)]
    dot_general x6 -> x0, matrix products: 19.5 us -> none  [the longest x2 7.83 us: per_device(): jnp.einsum('btk,btd->kd', windows_list[strand_index], grad_pres[strand_in...]
  transfers between devices with their start and end apart: 31 -> 0, of which waited for: 12 -> 0; matrix products, arithmetic and copies ran while one was open for 43% -> 0% of each run, Pallas kernels for 0% -> 0%
where the time goes in v1:
time: 103 us; the launch traced here: 102 us
  Pallas kernels  94.2 us (91%)
  local copies, waits for them, and re-layouts  7.5 us (7%)
    pallas_call x1, Pallas kernels, per_device(): pl.pallas_call(kernel, out_shape=(jax.ShapeDtypeStruct((OWN, C), BF), jax...  94.2 us
    unnamed x9, local copies, waits for them, and re-layouts  3.08 us

profile of v1, /device:TPU:1, one launch (start us, length us, event | category | flops | bytes accessed | tf_op | source)
XLA Modules:
  0.0 102.3 jit_solution(9232735660068401087)
XLA Ops:
  0.6 0.0 copy-start.2
  0.6 1.3 %reshape.18.gain = f32[1,768]{1,0:T(1,128)} reshape(f32[768]{0:T(1024)} %param.8) | data formatting | bytes 6144 | tf_op jit(solution)/shard_map/reshape | solution.py:579
  1.9 0.0 copy-done.2
  1.9 0.6 reshape.19.pairing
  2.5 0.7 pad.4
  3.3 0.6 copy.11
  3.9 94.2 %strands.1 = (bf16[128,768]{1,0:T(8,128)(2,1)}, bf16[128,768]{1,0:T(8,128)(2,1)}, f32[16,768]{1,0:T(8,128)}, f32[8,128]{1,0:T(8,128)}) custom-call(bf16[1,128,768]{2,1,0:T(8,128)(2,1)} %act.1, bf16[1,128,768]{2,1,0:T(8,128)(2,1)} %cot.1, bf16[2,3,16,128]{3,2,1,0:T(8,128)(2,1)} %bitcast.10, f32[1,768]{1,0:T(1,128)} %reshape.18.gain, s32[1,768]{1,0:T(1,128)} %reshape.19.pairing), custom_call_target="tpu_custom_call" | custom-call | tf_op jit(solution)/shard_map/strands/pallas_call | solution.py:564
  98.1 1.2 %slice_bitcast_fusion = f32[3]{0:T(128)} fusion(f32[8,128]{1,0:T(8,128)} %get-tuple-element.11), kind=kLoop, calls=%fused_computation.1 | loop fusion | bytes 24 | tf_op jit(solution)/shard_map/squeeze | solution.py:580
  99.3 0.0 copy-start
  99.3 1.7 %copy.15 = bf16[1,128,768]{2,1,0:T(8,128)(2,1)} copy(bf16[1,128,768]{2,1,0:T(8,128)(2,1)} %bitcast.9) | data formatting | bytes 393216
  100.9 0.0 copy-done
  100.9 0.0 copy-start.1
  100.9 0.7 copy.16
  101.6 0.1 copy-done.1
  101.7 0.6 copy.17
  (1 shorter events, 0.0 us)
Async XLA Ops:
  0.6 1.3 %copy-start.2 = (s32[768]{0:T(1024)S(1)}, s32[768]{0:T(1024)}, u32[]{:S(2)}) copy-start(s32[768]{0:T(1024)} %param.9) | copy-start | bytes 9220
  99.3 1.7 %copy-start = (bf16[128,768]{1,0:T(8,128)(2,1)S(1)}, bf16[128,768]{1,0:T(8,128)(2,1)}, u32[]{:S(2)}) copy-start(bf16[128,768]{1,0:T(8,128)(2,1)} %get-tuple-element.9) | copy-start | bytes 589828
  100.9 0.8 copy-start.1

commit v2 on v1

v2 whole, which is shorter than its diff:
```python
import functools

import jax
import jax.numpy as jnp
from jax import lax
from jax.experimental import pallas as pl
from jax.experimental.pallas import tpu as pltpu
from jax.sharding import PartitionSpec as P

EPS = 1e-06
MESH = pl.DeviceIdType.MESH
BF = jnp.bfloat16
F32 = jnp.float32

C = 768
HALF = 384
OWN = 128
TAPS = 5
ROWS = 288
CHIP0 = 16
NZ, NX, NY = 8, 4, 4
MSGS = 128
PHASES = 112


def rem(a, n):
    return lax.rem(a, jnp.int32(n))


def div(a, n):
    return lax.div(a, jnp.int32(n))


def place(z, x, y, c):
    return (z * 4 + div(x, 2) * 2 + c, rem(x, 2) * 4 + y)


def loop(count, body):
    def step(i, carry):
        body(i)
        return carry

    lax.fori_loop(0, count, step, 0)


def dot(a, b):
    return jnp.dot(a, b, preferred_element_type=F32)


def dot_nt(a, b):
    return lax.dot_general(a, b, (((1,), (1,)), ((), ())), preferred_element_type=F32)


def gelu_parts(x):
    k = 0.7978845608028654
    x2 = x * x
    t = jnp.tanh(k * (x + 0.044715 * x2 * x))
    cdf = 0.5 * (1.0 + t)
    slope = cdf + x * (0.5 * (1.0 - t * t)) * (k * (1.0 + 3 * 0.044715 * x2))
    return x * cdf, slope


def kernel(
    act, cot, wshard, gain, pairing,
    out_ref, grad_ref, gk_ref, gg_ref,
    xe, ce, xp, cp, perm, inv_ref, nf, wnd, wp, wpt, wb, dwb, acc,
    resf, resr, gpf, gpb, wun, gnb, gnx, rfx, rrx,
    slot4, slot8, red4, red8, slot_y, slot_x, slot_2x, one01, one2, slot_z, slot_2y,
    gsum, gz, gx, gy, gp_, fin, finx, spread, gather, same, wpad, wsh,
    send, recv, local, halo,
):
    s = lax.axis_index("seq")
    d = lax.axis_index("dp")
    z, xh, core = div(s, 4), rem(div(s, 2), 2), rem(s, 2)
    xl, y = div(d, 4), rem(d, 4)
    x = xh * 2 + xl
    m = z * 2 + xh
    other = 1 - core
    near = div(z, 4) * 4
    far = 4 - near

    def in_x(o):
        return place(z, rem(x + o, NX), y, core)

    def in_y(o):
        return place(z, x, rem(y + o, NY), core)

    def in_z(o):
        return place(rem(z + o, NZ), x, y, core)

    partner = place(z, x, y, other)

    def chip_m(mm, c):
        return place(div(mm, 2), rem(mm, 2) * 2 + xl, y, c)

    def iota(shape, axis):
        return lax.broadcasted_iota(jnp.int32, shape, axis)

    def onehot(flag):
        return flag.astype(F32).astype(BF)

    barrier = pltpu.get_barrier_semaphore()
    met = [partner]
    met += [in_x(o) for o in range(1, NX)] + [in_y(o) for o in range(1, NY)]
    met += [in_z(o) for o in range(1, NZ)]
    met += [chip_m(rem(m + o, 16), c) for o in (1, 15) for c in (0, 1)]
    for who in met:
        pl.semaphore_signal(barrier, inc=1, device_id=who, device_id_type=MESH)

    started = []

    def put(src, dst, who):
        i = len(started)
        copy = pltpu.make_async_remote_copy(
            src_ref=src, dst_ref=dst, send_sem=send.at[i], recv_sem=recv.at[i],
            device_id=who, device_id_type=MESH,
        )
        copy.start()
        started.append(copy)
        return copy

    def keep(src, dst, i):
        copy = pltpu.make_async_copy(src, dst, local.at[i])
        copy.start()
        return copy

    mine16 = pl.ds(pl.multiple_of(core * 16, 16), 16)
    mine = pl.ds(pl.multiple_of(CHIP0 + core * OWN, 16), OWN)
    half_cols = pl.ds(pl.multiple_of(core * HALF, 128), HALF)
    other_cols = pl.ds(pl.multiple_of(other * HALF, 128), HALF)

    x_here = keep(act.at[0], xe.at[mine], 1)
    c_here = keep(cot.at[0], ce.at[mine], 2)

    wpad[0:15, :] = wshard[...].astype(F32)
    wpad[15:16, :] = jnp.zeros((1, C), F32)
    for h in range(2):
        for j in range(3):
            first = h * HALF + j * 128
            wsh[h, j] = wpad[:, first : first + 128].astype(BF)

    perm[...] = onehot(iota((C, C), 0) == pairing[...])

    def source_of(slot):
        r = slot & 15
        c, yy, xx = (slot >> 4) & 1, (slot >> 5) & 3, slot >> 7
        return jnp.where(r < 15, ((c * 2 + xx) * 4 + yy) * 15 + r, -PHASES)

    spread[...] = onehot(iota((PHASES + 384, 256), 0) == source_of(iota((PHASES + 384, 256), 1)) + PHASES)
    gather[...] = onehot(iota((240, 256), 0) == source_of(iota((240, 256), 1)))
    same[...] = onehot(iota((256, 256), 0) == iota((256, 256), 1))
    nf[:, 0:8, :] = jnp.zeros((2, 8, C), F32)
    nf[:, 8 + ROWS :, :] = jnp.zeros((2, 8, C), F32)
    wnd[:, TAPS * C :] = jnp.zeros((2 * ROWS, 128), BF)
    gpf[:, 0:8, :] = jnp.zeros((2, 8, HALF), F32)
    gpf[:, 8 + ROWS :, :] = jnp.zeros((2, 8, HALF), F32)
    gsum[...] = jnp.zeros((8, 128), F32)

    pl.semaphore_wait(barrier, len(met))

    w_there = put(wsh.at[other], wb.at[:, z, x, y, mine16, :], partner)
    w_here = keep(wsh.at[core], wb.at[:, z, x, y, mine16, :], 0)
    edge_src = pl.ds(pl.multiple_of(core * 112, 16), 16)
    edge_dst = pl.ds(pl.multiple_of(other * 272, 16), 16)
    toward = rem(m + core * 2 + 15, 16)
    edges = []
    for c in (0, 1):
        for k, (src, dst) in enumerate(((act, xe), (cot, ce))):
            i = len(edges)
            copy = pltpu.make_async_remote_copy(
                src_ref=src.at[0, edge_src], dst_ref=dst.at[edge_dst],
                send_sem=halo.at[2 + i, 0], recv_sem=halo.at[k, core],
                device_id=chip_m(toward, c), device_id_type=MESH,
            )
            copy.start()
            edges.append(copy)
    x_there = put(act.at[0], xe.at[mine], partner)
    c_there = put(cot.at[0], ce.at[mine], partner)

    todo = []

    def fill(count):
        for _ in range(min(count, len(todo))):
            todo.pop(0)()

    def later(count, pieces, body):
        each = count // pieces
        for k in range(pieces):
            todo.append(lambda k=k: loop(each, lambda i: body(i + k * each)))

    def inside(first, count, width):
        row = iota((count, width), 0) + first
        low = jnp.where(m > 0, 0, CHIP0)
        high = jnp.where(m < 15, ROWS, ROWS - 16)
        return (row >= low) & (row < high)

    def swap_x():
        xp[...] = dot(xe[...], perm[...]).astype(BF)

    def swap_c():
        cp[...] = dot(ce[...], perm[...]).astype(BF)

    def norm_rows(i):
        at = pl.ds(pl.multiple_of(i * 32, 32), 32)
        live_rows = inside(i * 32, 32, C)
        values = jnp.where(live_rows, xe[at, :].astype(F32), 0.0)
        swapped = jnp.where(live_rows, xp[at, :].astype(F32), 0.0)
        inverse = lax.rsqrt(jnp.mean(values * values, -1, keepdims=True) + EPS)
        inv_ref[at, :] = inverse
        into = pl.ds(pl.multiple_of(8 + i * 32, 8), 32)
        nf[0, into, :] = (values * inverse * gain[...]).astype(BF).astype(F32)
        nf[1, into, :] = (swapped * inverse * gain[...]).astype(BF).astype(F32)

    def window_cols(i):
        cols = pl.ds(pl.multiple_of(i * 128, 128), 128)
        for strand in (0, 1):
            for k in range(TAPS):
                shift = (k - 2) if strand == 0 else (2 - k)
                into = pl.ds(pl.multiple_of(k * C + i * 128, 128), 128)
                wnd[strand * ROWS : (strand + 1) * ROWS, into] = nf[
                    strand, 8 + shift : 8 + shift + ROWS, cols
                ].astype(BF)

    def pad_group(g):
        cols = pl.ds(pl.multiple_of(div(15 * g, 8) * 128, 128), 384)
        right = spread[pl.ds(pl.multiple_of(PHASES - 16 * rem(15 * g, 8), 16), 384), :]
        into = pl.ds(pl.multiple_of(g * 256, 256), 256)
        wp[:, into] = dot(wnd[:, cols], right).astype(BF)

    def pad_group_t(g):
        at = pl.ds(pl.multiple_of(g * 256, 256), 256)
        for strand in (0, 1):
            rows = slice(strand * ROWS + CHIP0, strand * ROWS + CHIP0 + 256)
            wpt[at, strand * 256 : (strand + 1) * 256] = dot_nt(same[...], wp[rows, at]).astype(BF)

    todo.append(swap_x)
    todo.append(swap_c)
    later(9, 3, norm_rows)
    later(6, 3, window_cols)
    later(16, 8, pad_group)
    later(16, 8, pad_group_t)

    w_here.wait()
    w_there.wait_recv()
    first01 = [
        put(wb.at[pl.ds(0, 2), z, x, y], wb.at[pl.ds(0, 2), z, x, y], in_z(o)) for o in (4, 3, 5, 2, 6, 1, 7)
    ]
    first2 = [put(wb.at[2, z, x, y], wb.at[2, z, x, y], in_y(o)) for o in range(1, NY)]

    x_here.wait()
    c_here.wait()
    x_there.wait_recv()
    c_there.wait_recv()
    for copy in first2:
        copy.wait_recv()
    second2 = [put(wb.at[2, z, x], wb.at[2, z, x], in_x(o)) for o in range(1, NX)]
    for k, dst in enumerate((xe, ce)):
        for side in (0, 1):
            into = dst.at[pl.ds(272 * (1 - side), 16)]
            pltpu.make_async_remote_copy(
                src_ref=into, dst_ref=into, send_sem=halo.at[2, 0], recv_sem=halo.at[k, side],
                device_id=partner, device_id_type=MESH,
            ).wait_recv()

    def part(ref, colour, coord, half):
        if colour == 2:
            return ref.at[2, coord, pl.ds(half * 2, 2)]
        planes = pl.ds(far if half == 0 else near, 4)
        return ref.at[0, planes, coord] if colour == 0 else ref.at[1, planes, :, coord]

    rings = ((x, NX, in_x), (y, NY, in_y), (z, NZ, in_z))
    ways = ((1, 0), (-1, 1), (1, 1), (-1, 0))

    def limit(n, sign, half):
        return n // 2 if (half == 0) == (sign == 1) else n // 2 - 1

    def ring_send(colour, sign, half, hop):
        q, n, who = rings[colour]
        held = part(wb, colour, rem(q - sign * (hop - 1) + n, n), half)
        return put(held, held, who(1 if sign == 1 else n - 1))

    live = {}

    def ring_start(colour):
        for sign, half in ways:
            live[colour, sign, half] = ring_send(colour, sign, half, 1)

    def ring_hop(colour, hop, pieces):
        n = rings[colour][1]
        for sign, half in ways:
            if hop > limit(n, sign, half):
                continue
            live[colour, sign, half].wait_recv()
            if hop < limit(n, sign, half):
                live[colour, sign, half] = ring_send(colour, sign, half, hop + 1)
            fill(pieces)

    fill(1)
    for copy in first01:
        copy.wait_recv()
    second0 = [put(wb.at[0, :, x, y], wb.at[0, :, x, y], in_y(o)) for o in range(1, NY)]
    second1 = [put(wb.at[1, :, x, y], wb.at[1, :, x, y], in_x(o)) for o in range(1, NX)]
    fill(1)
    for copy in second2:
        copy.wait_recv()
    ring_start(2)
    fill(5)
    for copy in second0:
        copy.wait_recv()
    ring_start(0)
    for copy in second1:
        copy.wait_recv()
    ring_start(1)
    fill(4)
    ring_hop(2, 1, 0)
    fill(1)
    ring_hop(2, 2, 0)
    ring_hop(0, 1, 0)
    ring_hop(1, 1, 0)
    fill(2)
    ring_hop(2, 3, 1)
    fill(len(todo))
    ring_hop(0, 2, 0)
    ring_hop(1, 2, 0)
    ring_hop(2, 4, 0)

    def right_of(zz, count):
        return jnp.concatenate(
            [wb[j, pl.ds(zz, count)].reshape(count * 512, 128) for j in range(3)], axis=1
        )

    def left_of(zz, count):
        return wp[:, pl.ds(pl.multiple_of(zz * 512, 512), count * 512)]

    acc[...] = dot(left_of(0, 2), right_of(0, 2))

    def forward_step(i):
        acc[...] += dot(left_of(i * 2 + 2, 2), right_of(i * 2 + 2, 2))

    loop(3, forward_step)

    def gelu_rows(strand):
        def body(i):
            at = pl.ds(pl.multiple_of(i * 32, 32), 32)
            pre = acc[pl.ds(pl.multiple_of(strand * ROWS + i * 32, 32), 32), :]
            value, slope = gelu_parts(pre)
            if strand == 0:
                resf[at, :] = xe[at, half_cols].astype(F32) + value
                g = ce[at, half_cols].astype(F32)
            else:
                resr[at, :] = (xp[at, half_cols].astype(F32) + value).astype(BF)
                g = cp[at, half_cols].astype(F32)
            gp = jnp.where(inside(i * 32, 32, HALF), 0.5 * g * slope, 0.0).astype(BF)
            gpb[strand, at, :] = gp
            gpf[strand, pl.ds(pl.multiple_of(8 + i * 32, 8), 32), :] = gp.astype(F32)

        return body

    loop(ROWS // 32, gelu_rows(0))
    loop(ROWS // 32, gelu_rows(1))

    def dw_pair(p):
        right = jnp.concatenate(
            [gpb[0, CHIP0 : CHIP0 + 256, :], gpb[1, CHIP0 : CHIP0 + 256, :]], axis=0
        )
        got = dot(wpt[pl.ds(pl.multiple_of(p * 1024, 1024), 1024), :], right).astype(BF)
        for j in range(3):
            dwb[j, pl.ds(p * 2, 2)] = got[:, j * 128 : (j + 1) * 128].reshape(2, NX, NY, 32, 128)

    def ring_slot(colour, sign, half, dist):
        way = ways.index((sign, half))
        if colour == 2:
            return slot8.at[way, dist - 1]
        return slot4.at[colour, way, dist - 1]

    def ring_give(colour, sign, half, dist, src):
        q, n, who = rings[colour]
        return put(src, ring_slot(colour, sign, half, dist), who(1 if sign == 1 else n - 1))

    def ring_open(colour, sign, half):
        q, n, who = rings[colour]
        dist = limit(n, sign, half)
        src = part(dwb, colour, rem(q + sign * dist + n, n), half)
        live[colour, sign, half] = ring_give(colour, sign, half, dist, src)

    own_pair = div(z, 2)
    far_pair = rem(own_pair + 2, 4)
    dw_pair(far_pair)
    ring_open(2, 1, 0)
    ring_open(2, -1, 1)
    dw_pair(far_pair + 1 - 2 * rem(far_pair, 2))
    for colour in (0, 1):
        ring_open(colour, 1, 0)
        ring_open(colour, -1, 0)
    dw_pair(own_pair + 1 - 2 * rem(own_pair, 2))
    dw_pair(own_pair)
    ring_open(2, 1, 1)
    ring_open(2, -1, 0)
    for colour in (0, 1):
        ring_open(colour, 1, 1)
        ring_open(colour, -1, 1)

    there = pl.ds(pl.multiple_of(CHIP0 + other * OWN, 16), OWN)
    f_there = put(resf.at[there], rfx, partner)
    r_there = put(resr.at[there], rrx, partner)

    def pack_group(g):
        zz, hh = div(g, 2), rem(g, 2) * 2
        right = jnp.concatenate(
            [wb[j, zz, pl.ds(hh, 2)].reshape(256, 128) for j in range(3)], axis=1
        )
        wun[pl.ds(pl.multiple_of(g * 240, 16), 240), :] = dot(gather[...], right).astype(BF)

    def normed_grad(block, strand):
        first = 8 + CHIP0 + block * OWN
        total = None
        for k in range(TAPS):
            shift = (2 - k) if strand == 0 else (k - 2)
            left = gpf[strand, first + shift : first + shift + OWN, :].astype(BF)
            term = dot_nt(left, wun[k * C : (k + 1) * C, :])
            total = term if total is None else total + term
        gnb[block, strand] = total

    later(16, 4, pack_group)
    for block in (0, 1):
        for strand in (0, 1):
            todo.append(functools.partial(normed_grad, block, strand))

    def give_normed():
        live["gn"] = put(gnb.at[other], gnx, partner)

    todo.append(give_normed)

    def ring_step(colour, hop, pieces):
        q, n, who = rings[colour]
        for sign, half in ways:
            dist = limit(n, sign, half) - (hop - 1)
            if dist < 1:
                continue
            live[colour, sign, half].wait_recv()
            if dist > 1:
                got = ring_slot(colour, sign, half, dist)
                add = part(dwb, colour, rem(q + sign * (dist - 1) + n, n), half)
                got[...] = (got[...].astype(F32) + add[...].astype(F32)).astype(BF)
                live[colour, sign, half] = ring_give(colour, sign, half, dist - 1, got)
            fill(pieces)

    def ring_total(colour, half):
        q = rings[colour][0]
        total = part(dwb, colour, q, half)[...].astype(F32)
        for sign in (1, -1):
            total = total + ring_slot(colour, sign, half, 1)[...].astype(F32)
        return total.astype(BF)

    def finish_gain():
        live["gn"].wait_recv()
        at = mine
        inverse = inv_ref[at, :]
        v, vp = xe[at, :].astype(F32), xp[at, :].astype(F32)
        gn = gnb[core, 0] + gnx[0]
        gr = gnb[core, 1] + gnx[1]
        gnb[core, 0] = gn
        gnb[core, 1] = gr
        gain_part = jnp.sum(gn * v * inverse + gr * vp * inverse, 0, keepdims=True)
        for j in range(C // 128):
            gsum[j : j + 1, :] = gain_part[:, j * 128 : (j + 1) * 128]
        live["to_z"] = [put(gsum, gz.at[o - 1], in_z(o)) for o in range(1, NZ)]

    def finish_grad():
        at = mine
        inverse = inv_ref[at, :]
        cube = inverse * inverse * inverse
        v, vp = xe[at, :].astype(F32), xp[at, :].astype(F32)
        sf, sr = gnb[core, 0] * gain[...], gnb[core, 1] * gain[...]
        grad_r = 0.5 * cp[at, :].astype(F32) + inverse * sr - vp * (cube * jnp.mean(sr * vp, -1, keepdims=True))
        back = dot(grad_r.astype(BF), perm[...])
        grad_f = 0.5 * ce[at, :].astype(F32) + inverse * sf - v * (cube * jnp.mean(sf * v, -1, keepdims=True))
        grad_ref[...] = (grad_f + back).astype(BF)

    def finish_out():
        f_there.wait_recv()
        r_there.wait_recv()
        low = core == 0
        mine_f, their_f = resf[mine, :], rfx[...]
        mr, tr = resr[mine, :].astype(F32), rrx[...].astype(F32)
        full_r = jnp.concatenate([jnp.where(low, mr, tr), jnp.where(low, tr, mr)], axis=1)
        back_r = dot(full_r.astype(BF), perm[...])
        full_f = jnp.concatenate(
            [jnp.where(low, mine_f, their_f), jnp.where(low, their_f, mine_f)], axis=1
        )
        out_ref[...] = (0.5 * (full_f + back_r)).astype(BF)

    todo.append(finish_out)
    todo.append(finish_gain)
    todo.append(finish_grad)

    def gathered(own, slots):
        total = own
        for one in slots:
            total = total + one
        return total

    fill(5)
    ring_step(2, 1, 0)
    fill(1)
    ring_step(0, 1, 0)
    ring_step(1, 1, 0)
    fill(1)
    ring_step(2, 2, 0)
    fill(2)
    ring_step(0, 2, 0)
    ring_step(1, 2, 0)
    planes = (pl.ds(far, 4), pl.ds(near, 4))
    for colour in (0, 1):
        for half in (0, 1):
            red4[colour, planes[half]] = ring_total(colour, half)
    part0 = [put(red4.at[0, :, rem(y + o, NY)], slot_y.at[o - 1], in_y(o)) for o in range(1, NY)]
    part1 = [put(red4.at[1, :, rem(x + o, NX)], slot_x.at[o - 1], in_x(o)) for o in range(1, NX)]
    ring_step(2, 3, 0)
    fill(2)
    ring_step(2, 4, 0)
    red8[0:2] = ring_total(2, 0)
    red8[2:4] = ring_total(2, 1)
    part2 = [put(red8.at[rem(x + o, NX)], slot_2x.at[o - 1], in_x(o)) for o in range(1, NX)]
    fill(len(todo))

    for copy in part0 + part1:
        copy.wait_recv()
    one01[:, 0] = gathered(
        red4[0, :, y].astype(F32), [slot_y[o].astype(F32) for o in range(NY - 1)]
    ).astype(BF)
    one01[:, 1] = gathered(
        red4[1, :, x].astype(F32), [slot_x[o].astype(F32) for o in range(NX - 1)]
    ).astype(BF)
    last01 = [
        put(one01.at[rem(z + o, NZ)], slot_z.at[o - 1], in_z(o)) for o in (4, 3, 5, 2, 6, 1, 7)
    ]

    for copy in live["to_z"]:
        copy.wait_recv()
    gp_[0] = gathered(gsum[...], [gz[o] for o in range(NZ - 1)])
    to_x = [put(gp_.at[0], gx.at[o - 1], in_x(o)) for o in range(1, NX)]

    for copy in part2:
        copy.wait_recv()
    one2[...] = gathered(
        red8[x].astype(F32), [slot_2x[o].astype(F32) for o in range(NX - 1)]
    ).astype(BF)
    last2 = [put(one2.at[rem(y + o, NY)], slot_2y.at[o - 1], in_y(o)) for o in range(1, NY)]

    for copy in to_x:
        copy.wait_recv()
    gp_[1] = gathered(gp_[0], [gx[o] for o in range(NX - 1)])
    to_y = [put(gp_.at[1], gy.at[o - 1], in_y(o)) for o in range(1, NY)]
    for copy in last2:
        copy.wait_recv()
    fin[:, 256:384] = gathered(
        one2[y].astype(F32), [slot_2y[o].astype(F32) for o in range(NY - 1)]
    )
    for copy in last01:
        copy.wait_recv()
    for j in (0, 1):
        fin[:, j * 128 : (j + 1) * 128] = gathered(
            one01[z, j].astype(F32), [slot_z[o, j].astype(F32) for o in range(NZ - 1)]
        )
    theirs16 = pl.ds(pl.multiple_of(other * 16, 16), 16)
    fin_there = put(fin.at[theirs16], finx, partner)
    for copy in to_y:
        copy.wait_recv()
    gp_[2] = gathered(gp_[1], [gy[o] for o in range(NY - 1)])
    gain_there = put(gp_.at[2], gp_.at[3], partner)
    gk_ref[:, half_cols] = fin[mine16, :]
    fin_there.wait_recv()
    gk_ref[:, other_cols] = finx[...]
    gain_there.wait_recv()
    total = gp_[2] + gp_[3]
    flat = iota((8, 128), 0) * 128 + iota((8, 128), 1)
    picked = jnp.zeros((8, 128), F32)
    for j in range(3):
        chosen = jnp.where(flat == (s * 8 + d) * 3 + j, total, 0.0)
        value = jnp.sum(jnp.sum(chosen, 1, keepdims=True), 0, keepdims=True)
        picked = jnp.where(iota((8, 128), 1) == j, value, picked)
    gg_ref[...] = picked

    for copy in started:
        copy.wait_send()
    for copy in edges:
        copy.wait_send()


def scratch():
    v = pltpu.VMEM
    dma = pltpu.SemaphoreType.DMA
    return [
        v((ROWS, C), BF), v((ROWS, C), BF), v((ROWS, C), BF), v((ROWS, C), BF),
        v((C, C), BF), v((ROWS, 1), F32),
        v((2, ROWS + 16, C), F32), v((2 * ROWS, TAPS * C + 128), BF),
        v((2 * ROWS, 4096), BF), v((4096, 512), BF),
        v((3, NZ, NX, NY, 32, 128), BF), v((3, NZ, NX, NY, 32, 128), BF),
        v((2 * ROWS, HALF), F32), v((ROWS, HALF), F32), v((ROWS, HALF), BF),
        v((2, ROWS + 16, HALF), F32), v((2, ROWS, HALF), BF),
        v((TAPS * C, HALF), BF),
        v((2, 2, OWN, C), F32), v((2, OWN, C), F32),
        v((OWN, HALF), F32), v((OWN, HALF), BF),
        v((2, 4, 2, 4, 4, 32, 128), BF), v((4, 4, 2, NY, 32, 128), BF),
        v((2, NZ, 4, 32, 128), BF), v((NX, NY, 32, 128), BF),
        v((3, NZ, 32, 128), BF), v((3, NZ, 32, 128), BF),
        v((3, NY, 32, 128), BF),
        v((NZ, 2, 32, 128), BF), v((NY, 32, 128), BF),
        v((7, 2, 32, 128), BF), v((3, 32, 128), BF),
        v((8, 128), F32), v((7, 8, 128), F32), v((3, 8, 128), F32), v((3, 8, 128), F32),
        v((4, 8, 128), F32),
        v((32, HALF), F32), v((16, HALF), F32),
        v((PHASES + 384, 256), BF), v((240, 256), BF), v((256, 256), BF),
        v((16, C), F32), v((2, 3, 16, 128), BF),
        dma((MSGS,)), dma((MSGS,)), dma((3,)), dma((6, 2)),
    ]


def per_device(activations, cotangent, weights, norm_gain, pairing):
    vmem = pl.BlockSpec(memory_space=pltpu.VMEM)
    anywhere = pl.BlockSpec(memory_space=pl.ANY)
    combined, grad_input, grad_kernel, grad_gain = pl.pallas_call(
        kernel,
        out_shape=(
            jax.ShapeDtypeStruct((OWN, C), BF),
            jax.ShapeDtypeStruct((OWN, C), BF),
            jax.ShapeDtypeStruct((16, C), F32),
            jax.ShapeDtypeStruct((8, 128), F32),
        ),
        in_specs=[anywhere, anywhere, vmem, vmem, vmem],
        out_specs=(vmem, vmem, vmem, vmem),
        scratch_shapes=scratch(),
        compiler_params=pltpu.CompilerParams(
            collective_id=0, has_side_effects=True, vmem_limit_bytes=60 * 2**20
        ),
        name="strands",
    )(activations, cotangent, weights, norm_gain.reshape(1, C), pairing.reshape(1, C))
    return combined[None], grad_input[None], grad_kernel[:15], grad_gain[0, :3]


def solution(mesh):
    placed = (P("dp", "seq", None), P("dp", "seq", None), P(("seq", "dp"), None), P(), P())
    return jax.shard_map(
        per_device,
        mesh=mesh,
        in_specs=placed,
        out_specs=(
            P("dp", "seq", None),
            P("dp", "seq", None),
            P(("seq", "dp"), None),
            P(("seq", "dp")),
        ),
        check_vma=False,
    )
```

time: 103 us -> 84.6 us (0.82)
  Pallas kernels: 94.2 us -> 77.6 us
  local copies, waits for them, and re-layouts: 7.5 us -> 6.12 us
    pallas_call x1, Pallas kernels: 94.2 us -> 77.6 us  [per_device(): pl.pallas_call(kernel, out_shape=(jax.ShapeDtypeStruct((OWN, C), BF), jax...]
where the time goes in v2:
time: 84.6 us; the launch traced here: 84.3 us
  Pallas kernels  77.6 us (92%)
  local copies, waits for them, and re-layouts  6.12 us (7%)
    pallas_call x1, Pallas kernels, per_device(): pl.pallas_call(kernel, out_shape=(jax.ShapeDtypeStruct((OWN, C), BF), jax...  77.6 us
    unnamed x9, local copies, waits for them, and re-layouts  3.08 us

profile of v2, /device:TPU:1, one launch (start us, length us, event | category | flops | bytes accessed | tf_op | source)
XLA Modules:
  0.0 84.3 jit_solution(2032395438850164793)
XLA Ops:
  0.6 0.0 copy-start.2
  0.6 1.3 %reshape.14.gain = f32[1,768]{1,0:T(1,128)} reshape(f32[768]{0:T(1024)} %param.8) | data formatting | bytes 6144 | tf_op jit(solution)/shard_map/reshape | solution.py:638
  1.9 0.0 copy-done.2
  1.9 0.6 reshape.15.pairing
  2.5 77.6 %strands.1 = (bf16[128,768]{1,0:T(8,128)(2,1)}, bf16[128,768]{1,0:T(8,128)(2,1)}, f32[16,768]{1,0:T(8,128)}, f32[8,128]{1,0:T(8,128)}) custom-call(bf16[1,128,768]{2,1,0:T(8,128)(2,1)} %act.1, bf16[1,128,768]{2,1,0:T(8,128)(2,1)} %cot.1, bf16[15,768]{1,0:T(8,128)(2,1)} %wshard.1, f32[1,768]{1,0:T(1,128)} %reshape.14.gain, s32[1,768]{1,0:T(1,128)} %reshape.15.pairing), custom_call_target="tpu_custom_call" | custom-call | tf_op jit(solution)/shard_map/strands/pallas_call | solution.py:623
  80.1 1.2 %slice_bitcast_fusion = f32[3]{0:T(128)} fusion(f32[8,128]{1,0:T(8,128)} %get-tuple-element.11), kind=kLoop, calls=%fused_computation | loop fusion | bytes 24 | tf_op jit(solution)/shard_map/squeeze | solution.py:639
  81.2 0.0 copy-start
  81.2 1.7 %copy.12 = bf16[1,128,768]{2,1,0:T(8,128)(2,1)} copy(bf16[1,128,768]{2,1,0:T(8,128)(2,1)} %bitcast.6) | data formatting | bytes 393216
  82.9 0.0 copy-done
  82.9 0.0 copy-start.1
  82.9 0.7 copy.13
  83.6 0.1 copy-done.1
  83.7 0.6 copy.14
Async XLA Ops:
  0.6 1.3 %copy-start.2 = (s32[768]{0:T(1024)S(1)}, s32[768]{0:T(1024)}, u32[]{:S(2)}) copy-start(s32[768]{0:T(1024)} %param.9) | copy-start | bytes 9220
  81.2 1.7 %copy-start = (bf16[128,768]{1,0:T(8,128)(2,1)S(1)}, bf16[128,768]{1,0:T(8,128)(2,1)}, u32[]{:S(2)}) copy-start(bf16[128,768]{1,0:T(8,128)(2,1)} %get-tuple-element.9) | copy-start | bytes 589828
  82.9 0.8 copy-start.1

commit v3 on v2

--- a/solution.py
+++ b/solution.py
@@ -19,7 +19,7 @@
 ROWS = 288
 CHIP0 = 16
 NZ, NX, NY = 8, 4, 4
-MSGS = 128
+MSGS = 176
 PHASES = 112
 
 
@@ -66,7 +66,7 @@
     xe, ce, xp, cp, perm, inv_ref, nf, wnd, wp, wpt, wb, dwb, acc,
     resf, resr, gpf, gpb, wun, gnb, gnx, rfx, rrx,
     slot4, slot8, red4, red8, slot_y, slot_x, slot_2x, one01, one2, slot_z, slot_2y,
-    gsum, gz, gx, gy, gp_, fin, finx, spread, gather, same, wpad, wsh,
+    gsum, gz, gx, gy, gp_, fin, finx, spread, gather, wpad, wsh, gain2,
     send, recv, local, halo,
 ):
     s = lax.axis_index("seq")
@@ -139,7 +139,9 @@
             first = h * HALF + j * 128
             wsh[h, j] = wpad[:, first : first + 128].astype(BF)
 
-    perm[...] = onehot(iota((C, C), 0) == pairing[...])
+    gain_row = gain[...].reshape(1, C)
+    perm[...] = onehot(iota((C, C), 0) == pairing[...].reshape(1, C))
+    gain2[...] = gain_row
 
     def source_of(slot):
         r = slot & 15
@@ -148,7 +150,6 @@
 
     spread[...] = onehot(iota((PHASES + 384, 256), 0) == source_of(iota((PHASES + 384, 256), 1)) + PHASES)
     gather[...] = onehot(iota((240, 256), 0) == source_of(iota((240, 256), 1)))
-    same[...] = onehot(iota((256, 256), 0) == iota((256, 256), 1))
     nf[:, 0:8, :] = jnp.zeros((2, 8, C), F32)
     nf[:, 8 + ROWS :, :] = jnp.zeros((2, 8, C), F32)
     wnd[:, TAPS * C :] = jnp.zeros((2 * ROWS, 128), BF)
@@ -208,8 +209,8 @@
         inverse = lax.rsqrt(jnp.mean(values * values, -1, keepdims=True) + EPS)
         inv_ref[at, :] = inverse
         into = pl.ds(pl.multiple_of(8 + i * 32, 8), 32)
-        nf[0, into, :] = (values * inverse * gain[...]).astype(BF).astype(F32)
-        nf[1, into, :] = (swapped * inverse * gain[...]).astype(BF).astype(F32)
+        nf[0, into, :] = (values * inverse * gain2[...]).astype(BF).astype(F32)
+        nf[1, into, :] = (swapped * inverse * gain2[...]).astype(BF).astype(F32)
 
     def window_cols(i):
         cols = pl.ds(pl.multiple_of(i * 128, 128), 128)
@@ -231,7 +232,7 @@
         at = pl.ds(pl.multiple_of(g * 256, 256), 256)
         for strand in (0, 1):
             rows = slice(strand * ROWS + CHIP0, strand * ROWS + CHIP0 + 256)
-            wpt[at, strand * 256 : (strand + 1) * 256] = dot_nt(same[...], wp[rows, at]).astype(BF)
+            wpt[at, strand * 256 : (strand + 1) * 256] = wp[rows, at].T
 
     todo.append(swap_x)
     todo.append(swap_c)
@@ -240,27 +241,27 @@
     later(16, 8, pad_group)
     later(16, 8, pad_group_t)
 
+    second0, second1 = {}, {}
+
+    def forward_shard(o):
+        zz = rem(z + NZ - o, NZ)
+        held0, held1 = wb.at[0, zz, x, y], wb.at[1, zz, x, y]
+        second0[o] = [put(held0, held0, in_y(p)) for p in (2, 1, 3)]
+        second1[o] = [put(held1, held1, in_x(p)) for p in (2, 1, 3)]
+
     w_here.wait()
     w_there.wait_recv()
-    first01 = [
-        put(wb.at[pl.ds(0, 2), z, x, y], wb.at[pl.ds(0, 2), z, x, y], in_z(o)) for o in (4, 3, 5, 2, 6, 1, 7)
-    ]
-    first2 = [put(wb.at[2, z, x, y], wb.at[2, z, x, y], in_y(o)) for o in range(1, NY)]
-
-    x_here.wait()
-    c_here.wait()
-    x_there.wait_recv()
-    c_there.wait_recv()
-    for copy in first2:
-        copy.wait_recv()
-    second2 = [put(wb.at[2, z, x], wb.at[2, z, x], in_x(o)) for o in range(1, NX)]
-    for k, dst in enumerate((xe, ce)):
-        for side in (0, 1):
-            into = dst.at[pl.ds(272 * (1 - side), 16)]
-            pltpu.make_async_remote_copy(
-                src_ref=into, dst_ref=into, send_sem=halo.at[2, 0], recv_sem=halo.at[k, side],
-                device_id=partner, device_id_type=MESH,
-            ).wait_recv()
+    first2 = [put(wb.at[2, z, x, y], wb.at[2, z, x, y], in_y(o)) for o in (2, 1, 3)]
+    first01 = {
+        o: put(wb.at[pl.ds(0, 2), z, x, y], wb.at[pl.ds(0, 2), z, x, y], in_z(o))
+        for o in (4, 3, 5, 2, 6, 1, 7)
+    }
+    forward_shard(0)
+
+    def pass_on(*offsets):
+        for o in offsets:
+            first01[o].wait_recv()
+            forward_shard(o)
 
     def part(ref, colour, coord, half):
         if colour == 2:
@@ -295,30 +296,43 @@
                 live[colour, sign, half] = ring_send(colour, sign, half, hop + 1)
             fill(pieces)
 
+    for copy in first2:
+        copy.wait_recv()
+    second2 = [put(wb.at[2, z, x], wb.at[2, z, x], in_x(o)) for o in (2, 1, 3)]
+    pass_on(1, 7)
+    x_here.wait()
+    c_here.wait()
+    x_there.wait_recv()
+    c_there.wait_recv()
+    pass_on(2, 6)
+    for k, dst in enumerate((xe, ce)):
+        for side in (0, 1):
+            into = dst.at[pl.ds(272 * (1 - side), 16)]
+            pltpu.make_async_remote_copy(
+                src_ref=into, dst_ref=into, send_sem=halo.at[2, 0], recv_sem=halo.at[k, side],
+                device_id=partner, device_id_type=MESH,
+            ).wait_recv()
+    pass_on(3, 5)
     fill(1)
-    for copy in first01:
-        copy.wait_recv()
-    second0 = [put(wb.at[0, :, x, y], wb.at[0, :, x, y], in_y(o)) for o in range(1, NY)]
-    second1 = [put(wb.at[1, :, x, y], wb.at[1, :, x, y], in_x(o)) for o in range(1, NX)]
-    fill(1)
+    pass_on(4)
     for copy in second2:
         copy.wait_recv()
     ring_start(2)
-    fill(5)
-    for copy in second0:
-        copy.wait_recv()
+    fill(4)
+    for o in (0, 1, 7, 2, 6, 3, 5, 4):
+        for copy in second0[o] + second1[o]:
+            copy.wait_recv()
     ring_start(0)
-    for copy in second1:
-        copy.wait_recv()
     ring_start(1)
-    fill(4)
+    fill(3)
     ring_hop(2, 1, 0)
-    fill(1)
+    fill(3)
     ring_hop(2, 2, 0)
+    fill(2)
     ring_hop(0, 1, 0)
     ring_hop(1, 1, 0)
     fill(2)
-    ring_hop(2, 3, 1)
+    ring_hop(2, 3, 0)
     fill(len(todo))
     ring_hop(0, 2, 0)
     ring_hop(1, 2, 0)
@@ -411,39 +425,34 @@
         )
         wun[pl.ds(pl.multiple_of(g * 240, 16), 240), :] = dot(gather[...], right).astype(BF)
 
-    def normed_grad(block, strand):
-        first = 8 + CHIP0 + block * OWN
-        total = None
-        for k in range(TAPS):
-            shift = (2 - k) if strand == 0 else (k - 2)
-            left = gpf[strand, first + shift : first + shift + OWN, :].astype(BF)
-            term = dot_nt(left, wun[k * C : (k + 1) * C, :])
-            total = term if total is None else total + term
-        gnb[block, strand] = total
+    def normed_grad(k):
+        pieces = []
+        for block in (0, 1):
+            for strand in (0, 1):
+                first = 8 + CHIP0 + block * OWN + ((2 - k) if strand == 0 else (k - 2))
+                pieces.append(gpf[strand, first : first + OWN, :])
+        left = jnp.concatenate(pieces, axis=0).astype(BF)
+        term = dot_nt(left, wun[k * C : (k + 1) * C, :]).reshape(2, 2, OWN, C)
+        gnb[...] = term if k == 0 else gnb[...] + term
 
     later(16, 4, pack_group)
-    for block in (0, 1):
-        for strand in (0, 1):
-            todo.append(functools.partial(normed_grad, block, strand))
+    for k in range(TAPS):
+        todo.append(functools.partial(normed_grad, k))
 
     def give_normed():
         live["gn"] = put(gnb.at[other], gnx, partner)
 
     todo.append(give_normed)
 
-    def ring_step(colour, hop, pieces):
+    def serve(colour, way, dist):
         q, n, who = rings[colour]
-        for sign, half in ways:
-            dist = limit(n, sign, half) - (hop - 1)
-            if dist < 1:
-                continue
-            live[colour, sign, half].wait_recv()
-            if dist > 1:
-                got = ring_slot(colour, sign, half, dist)
-                add = part(dwb, colour, rem(q + sign * (dist - 1) + n, n), half)
-                got[...] = (got[...].astype(F32) + add[...].astype(F32)).astype(BF)
-                live[colour, sign, half] = ring_give(colour, sign, half, dist - 1, got)
-            fill(pieces)
+        sign, half = ways[way]
+        live[colour, sign, half].wait_recv()
+        if dist > 1:
+            got = ring_slot(colour, sign, half, dist)
+            add = part(dwb, colour, rem(q + sign * (dist - 1) + n, n), half)
+            got[...] = (got[...].astype(F32) + add[...].astype(F32)).astype(BF)
+            live[colour, sign, half] = ring_give(colour, sign, half, dist - 1, got)
 
     def ring_total(colour, half):
         q = rings[colour][0]
@@ -471,7 +480,7 @@
         inverse = inv_ref[at, :]
         cube = inverse * inverse * inverse
         v, vp = xe[at, :].astype(F32), xp[at, :].astype(F32)
-        sf, sr = gnb[core, 0] * gain[...], gnb[core, 1] * gain[...]
+        sf, sr = gnb[core, 0] * gain2[...], gnb[core, 1] * gain2[...]
         grad_r = 0.5 * cp[at, :].astype(F32) + inverse * sr - vp * (cube * jnp.mean(sr * vp, -1, keepdims=True))
         back = dot(grad_r.astype(BF), perm[...])
         grad_f = 0.5 * ce[at, :].astype(F32) + inverse * sf - v * (cube * jnp.mean(sf * v, -1, keepdims=True))
@@ -500,29 +509,45 @@
             total = total + one
         return total
 
-    fill(5)
-    ring_step(2, 1, 0)
+    fill(2)
+    serve(2, 0, 4)
+    serve(2, 1, 4)
     fill(1)
-    ring_step(0, 1, 0)
-    ring_step(1, 1, 0)
+    serve(0, 0, 2)
+    serve(1, 0, 2)
     fill(1)
-    ring_step(2, 2, 0)
-    fill(2)
-    ring_step(0, 2, 0)
-    ring_step(1, 2, 0)
+    serve(2, 2, 3)
+    serve(2, 3, 3)
+    fill(1)
+    serve(0, 1, 2)
+    serve(1, 1, 2)
+    fill(1)
+    serve(2, 0, 3)
+    serve(2, 1, 3)
+    fill(1)
+    serve(2, 2, 2)
+    serve(2, 3, 2)
+    fill(3)
     planes = (pl.ds(far, 4), pl.ds(near, 4))
+    for colour in (0, 1):
+        for way in range(4):
+            serve(colour, way, 1)
     for colour in (0, 1):
         for half in (0, 1):
             red4[colour, planes[half]] = ring_total(colour, half)
-    part0 = [put(red4.at[0, :, rem(y + o, NY)], slot_y.at[o - 1], in_y(o)) for o in range(1, NY)]
-    part1 = [put(red4.at[1, :, rem(x + o, NX)], slot_x.at[o - 1], in_x(o)) for o in range(1, NX)]
-    ring_step(2, 3, 0)
+    part0 = [put(red4.at[0, :, rem(y + o, NY)], slot_y.at[o - 1], in_y(o)) for o in (2, 1, 3)]
+    part1 = [put(red4.at[1, :, rem(x + o, NX)], slot_x.at[o - 1], in_x(o)) for o in (2, 1, 3)]
+    serve(2, 0, 2)
+    serve(2, 1, 2)
     fill(2)
-    ring_step(2, 4, 0)
+    serve(2, 2, 1)
+    serve(2, 3, 1)
+    fill(1)
+    serve(2, 0, 1)
+    serve(2, 1, 1)
     red8[0:2] = ring_total(2, 0)
     red8[2:4] = ring_total(2, 1)
-    part2 = [put(red8.at[rem(x + o, NX)], slot_2x.at[o - 1], in_x(o)) for o in range(1, NX)]
-    fill(len(todo))
+    part2 = [put(red8.at[rem(x + o, NX)], slot_2x.at[o - 1], in_x(o)) for o in (2, 1, 3)]
 
     for copy in part0 + part1:
         copy.wait_recv()
@@ -535,6 +560,7 @@
     last01 = [
         put(one01.at[rem(z + o, NZ)], slot_z.at[o - 1], in_z(o)) for o in (4, 3, 5, 2, 6, 1, 7)
     ]
+    fill(len(todo))
 
     for copy in live["to_z"]:
         copy.wait_recv()
@@ -546,7 +572,7 @@
     one2[...] = gathered(
         red8[x].astype(F32), [slot_2x[o].astype(F32) for o in range(NX - 1)]
     ).astype(BF)
-    last2 = [put(one2.at[rem(y + o, NY)], slot_2y.at[o - 1], in_y(o)) for o in range(1, NY)]
+    last2 = [put(one2.at[rem(y + o, NY)], slot_2y.at[o - 1], in_y(o)) for o in (2, 1, 3)]
 
     for copy in to_x:
         copy.wait_recv()
@@ -557,6 +583,10 @@
     fin[:, 256:384] = gathered(
         one2[y].astype(F32), [slot_2y[o].astype(F32) for o in range(NY - 1)]
     )
+    for copy in to_y:
+        copy.wait_recv()
+    gp_[2] = gathered(gp_[1], [gy[o] for o in range(NY - 1)])
+    gain_there = put(gp_.at[2], gp_.at[3], partner)
     for copy in last01:
         copy.wait_recv()
     for j in (0, 1):
@@ -565,10 +595,6 @@
         )
     theirs16 = pl.ds(pl.multiple_of(other * 16, 16), 16)
     fin_there = put(fin.at[theirs16], finx, partner)
-    for copy in to_y:
-        copy.wait_recv()
-    gp_[2] = gathered(gp_[1], [gy[o] for o in range(NY - 1)])
-    gain_there = put(gp_.at[2], gp_.at[3], partner)
     gk_ref[:, half_cols] = fin[mine16, :]
     fin_there.wait_recv()
     gk_ref[:, other_cols] = finx[...]
@@ -611,10 +637,18 @@
         v((8, 128), F32), v((7, 8, 128), F32), v((3, 8, 128), F32), v((3, 8, 128), F32),
         v((4, 8, 128), F32),
         v((32, HALF), F32), v((16, HALF), F32),
-        v((PHASES + 384, 256), BF), v((240, 256), BF), v((256, 256), BF),
-        v((16, C), F32), v((2, 3, 16, 128), BF),
+        v((PHASES + 384, 256), BF), v((240, 256), BF),
+        v((16, C), F32), v((2, 3, 16, 128), BF), v((1, C), F32),
         dma((MSGS,)), dma((MSGS,)), dma((3,)), dma((6, 2)),
     ]
+
+
+def hand_over(a, b, c, d, a_out, b_out, c_out, d_out):
+    a_out[0] = a[...]
+    b_out[0] = b[...]
+    c_out[...] = c[0:15, :]
+    for j in range(3):
+        d_out[j] = d[0, j]
 
 
 def per_device(activations, cotangent, weights, norm_gain, pairing):
@@ -635,8 +669,19 @@
             collective_id=0, has_side_effects=True, vmem_limit_bytes=60 * 2**20
         ),
         name="strands",
-    )(activations, cotangent, weights, norm_gain.reshape(1, C), pairing.reshape(1, C))
-    return combined[None], grad_input[None], grad_kernel[:15], grad_gain[0, :3]
+    )(activations, cotangent, weights, norm_gain, pairing)
+    return pl.pallas_call(
+        hand_over,
+        out_shape=(
+            jax.ShapeDtypeStruct((1, OWN, C), BF),
+            jax.ShapeDtypeStruct((1, OWN, C), BF),
+            jax.ShapeDtypeStruct((15, C), F32),
+            jax.ShapeDtypeStruct((3,), F32),
+        ),
+        in_specs=[vmem, vmem, vmem, vmem],
+        out_specs=(vmem, vmem, vmem, pl.BlockSpec(memory_space=pltpu.SMEM)),
+        name="results",
+    )(combined, grad_input, grad_kernel, grad_gain)
 
 
 def solution(mesh):

time: 84.6 us -> 76.9 us (0.909)
  local copies, waits for them, and re-layouts: 6.12 us -> 0 us
  Pallas kernels: 77.6 us -> 75.9 us
    pallas_call x1, Pallas kernels: 77.6 us -> 74.1 us  [per_device(): pl.pallas_call(kernel, out_shape=(jax.ShapeDtypeStruct((OWN, C), BF), jax...]
    unnamed x9 -> x0, local copies, waits for them, and re-layouts: 3.08 us -> none
    reshape x2 -> x0, local copies, waits for them, and re-layouts: 1.85 us -> none  [the longest x1 1.27 us: per_device(): norm_gain.reshape(1, C)]
    pallas_call x0 -> x1, Pallas kernels: none -> 1.8 us  [per_device(): pl.pallas_call(hand_over, out_shape=(jax.ShapeDtypeStruct((1, OWN, C), BF...]
    squeeze x1 -> x0, local copies, waits for them, and re-layouts: 1.19 us -> none  [per_device(): grad_gain[0, :3]]
where the time goes in v3:
time: 76.9 us; the launch traced here: 76.7 us
  Pallas kernels  75.9 us (99%)
  between operations  0.8 us (1%)
    pallas_call x1, Pallas kernels, per_device(): pl.pallas_call(kernel, out_shape=(jax.ShapeDtypeStruct((OWN, C), BF), jax...  74.1 us
    pallas_call x1, Pallas kernels, per_device(): pl.pallas_call(hand_over, out_shape=(jax.ShapeDtypeStruct((1, OWN, C), BF...  1.8 us

profile of v3, /device:TPU:1, one launch (start us, length us, event | category | flops | bytes accessed | tf_op | source)
XLA Modules:
  0.0 76.7 jit_solution(7322479236566405308)
XLA Ops:
  0.6 74.1 %strands.1 = (bf16[128,768]{1,0:T(8,128)(2,1)}, bf16[128,768]{1,0:T(8,128)(2,1)}, f32[16,768]{1,0:T(8,128)}, f32[8,128]{1,0:T(8,128)}) custom-call(bf16[1,128,768]{2,1,0:T(8,128)(2,1)} %act.1, bf16[1,128,768]{2,1,0:T(8,128)(2,1)} %cot.1, bf16[15,768]{1,0:T(8,128)(2,1)} %wshard.1, f32[768]{0:T(1024)} %gain.1, s32[768]{0:T(1024)} %pairing.1), custom_call_target="tpu_custom_call" | custom-call | tf_op jit(solution)/shard_map/strands/pallas_call | solution.py:657
  74.8 1.8 %results.1 = (bf16[1,128,768]{2,1,0:T(8,128)(2,1)}, bf16[1,128,768]{2,1,0:T(8,128)(2,1)}, f32[15,768]{1,0:T(8,128)}, f32[3]{0:T(128)}) custom-call(bf16[128,768]{1,0:T(8,128)(2,1)} %get-tuple-element.8.a, bf16[128,768]{1,0:T(8,128)(2,1)} %get-tuple-element.9.b, f32[16,768]{1,0:T(8,128)} %get-tuple-element.10.c, f32[8,128]{1,0:T(8,128)} %get-tuple-element.11.d), custom_call_target="tpu_custom_call" | custom-call | tf_op jit(solution)/shard_map/results/pallas_call | solution.py:673
